TPU v7x, 32 devices: a whole 2x2x4 slice. The times are simulated.
32 devices in a mesh: dp: 8 (over z, x), tensor: 4 (over y, core).
Axes of the slice: x: 2, y: 2, z: 4, core: 2. Of those that a mesh axis runs over, the one named last changes fastest.
Arguments:
- tokens: bfloat16 [4096, 1024], P(('dp', 'tensor')), may hold values from -6 to 6
- seg_starts: int32 [8, 6], P('dp'), may hold values from 1 to 511, as said below
- norm1_gain: float32 [1024], replicated, may hold values from 0.5 to 1.5
- w_mix: bfloat16 [1024, 8, 768], P(None, 'tensor'), may hold values from -0.1875 to 0.1875
- w_gates: bfloat16 [1024, 8, 2], P(None, 'tensor'), may hold values from -0.1875 to 0.1875
- conv_w: float32 [4, 8, 512], P(None, 'tensor'), may hold values from -3 to 3
- decay_rate: float32 [8], P('tensor'), may hold values from 0.001 to 0.1
- onorm_gain: float32 [8, 256], P('tensor'), may hold values from 0.5 to 1.5
- w_out: bfloat16 [8, 256, 1024], P('tensor'), may hold values from -0.25 to 0.25
- norm2_gain: float32 [1024], replicated, may hold values from 0.5 to 1.5
- w_gu: bfloat16 [1024, 2, 2816], P(None, None, 'tensor'), may hold values from -0.1875 to 0.1875
- w_down: bfloat16 [2816, 1024], P('tensor'), may hold values from -0.21875 to 0.21875
- cotangent: bfloat16 [4096, 1024], P(('dp', 'tensor')), may hold values from -6 to 6
Outputs:
- output: bfloat16 [4096, 1024], P(('dp', 'tensor'))
- grad_tokens: bfloat16 [4096, 1024], P(('dp', 'tensor'))
- grad_norm1_gain: float32 [1024], P('dp')
- grad_w_mix: float32 [1024, 8, 768], P('dp', 'tensor')
- grad_w_gates: float32 [1024, 8, 2], P('dp', 'tensor')
- grad_conv_w: float32 [4, 8, 512], P(None, 'tensor')
- grad_decay_rate: float32 [8], P('tensor')
- grad_onorm_gain: float32 [8, 256], P('tensor')
- grad_w_out: float32 [8, 256, 1024], P('tensor', None, 'dp')
- grad_norm2_gain: float32 [1024], P('dp')
- grad_w_gu: float32 [1024, 2, 2816], P('dp', None, 'tensor')
- grad_w_down: float32 [2816, 1024], P('tensor', 'dp')
Inputs may be any that keep to these rules, and one draw needn't show every extreme that they name: `seg_starts`: each entry is a position where a document begins in that sequence; every row names one position twice.
All inputs are finite; a program needn't handle non-finite values.
Results may differ from a plain program's by a relative error of at most 0.024.
Values may be sent and summed in bfloat16 or wider, within the bound.
A program may use at most 128 MiB of HBM per device.

v0:
```python
import jax
import jax.numpy as jnp
from jax import lax
from jax.sharding import PartitionSpec as P

BLOCK = 64


def rms_norm(rows, gain):
    return rows * lax.rsqrt(jnp.mean(rows * rows, axis=-1, keepdims=True) + 1e-06) * gain


def segment_ids(starts_row, length):
    places = jnp.arange(length, dtype=jnp.int32)
    flags = jnp.any(starts_row[:, None] == places[None, :], axis=0).astype(jnp.int32)
    seg = jnp.cumsum(flags)
    before = jnp.concatenate([seg[:1], seg[:-1]])
    return (seg, before)


def core(proj, gates_pre, conv_w, decay_rate, onorm_gain, seg, before):
    highest = lax.Precision.HIGHEST
    length, heads, width = proj.shape
    value_width = onorm_gain.shape[-1]
    conv_cols = conv_w.shape[-1]
    key_width = (conv_cols - value_width) // 2
    mixed = proj[:, :, :conv_cols]
    total = jnp.zeros_like(mixed)
    for lag in range(4):
        moved = jnp.pad(mixed, ((lag, 0), (0, 0), (0, 0)))[:length]
        moved_seg = jnp.pad(seg, (lag, 0), constant_values=-1)[:length]
        keep = (moved_seg == seg).astype(jnp.float32)
        total = total + conv_w[3 - lag][None] * moved * keep[:, None, None]
    act = jax.nn.silu(total)
    query = act[..., :key_width]
    keys = act[..., key_width : 2 * key_width]
    values = act[..., 2 * key_width :]
    query = (
        query
        * lax.rsqrt(jnp.sum(query * query, axis=-1, keepdims=True) + 1e-06)
        * key_width ** (-0.5)
    )
    keys = keys * lax.rsqrt(jnp.sum(keys * keys, axis=-1, keepdims=True) + 1e-06)
    gate_out = proj[..., conv_cols:]
    beta = jax.nn.sigmoid(gates_pre[..., 1])
    log_decay = -decay_rate[None, :] * jax.nn.softplus(gates_pre[..., 0])
    blocks = length // BLOCK

    def split(arr):
        return arr.reshape((blocks, BLOCK) + arr.shape[1:])

    items = (
        split(query),
        split(keys),
        split(values),
        split(beta),
        split(log_decay),
        split(seg),
        before.reshape(blocks, BLOCK)[:, 0],
    )
    places = jnp.arange(BLOCK)
    inclusive = places[:, None] >= places[None, :]
    strict = (places[:, None] > places[None, :]).astype(jnp.float32)
    unit = jnp.eye(BLOCK, dtype=jnp.float32)

    def step(state, item):
        q_blk, k_blk, v_blk, beta_blk, logd_blk, seg_blk, prev = item
        cum = jnp.cumsum(logd_blk, axis=0)
        live = jnp.logical_and(seg_blk[:, None] == seg_blk[None, :], inclusive)
        diff = cum.T[:, :, None] - cum.T[:, None, :]
        within = jnp.exp(jnp.where(live[None], diff, 0.0)) * live[None].astype(jnp.float32)
        carried = jnp.exp(cum) * (seg_blk == prev).astype(jnp.float32)[:, None]
        kk = jnp.einsum("thd,jhd->htj", k_blk, k_blk, precision=highest)
        lower = beta_blk.T[:, :, None] * within * kk * strict[None]
        start_val = jnp.einsum("thd,hde->hte", k_blk, state, precision=highest)
        rhs = beta_blk.T[:, :, None] * (
            jnp.transpose(v_blk, (1, 0, 2)) - carried.T[:, :, None] * start_val
        )
        errs = lax.linalg.triangular_solve(
            unit[None] + lower, rhs, left_side=True, lower=True, unit_diagonal=True
        )
        qk = jnp.einsum("thd,jhd->htj", q_blk, k_blk, precision=highest)
        read = carried.T[:, :, None] * jnp.einsum("thd,hde->hte", q_blk, state, precision=highest)
        read = read + jnp.einsum("htj,hje->hte", within * qk, errs, precision=highest)
        final_row = within[:, -1, :]
        new_state = carried[-1][:, None, None] * state + jnp.einsum(
            "hj,jhd,hje->hde", final_row, k_blk, errs, precision=highest
        )
        return (new_state, jnp.transpose(read, (1, 0, 2)))

    start_state = jnp.zeros((heads, key_width, value_width), jnp.float32)
    _, reads = lax.scan(step, start_state, items)
    outs = reads.reshape(length, heads, value_width)
    return (
        outs
        * lax.rsqrt(jnp.mean(outs * outs, axis=-1, keepdims=True) + 1e-05)
        * onorm_gain[None]
        * jax.nn.silu(gate_out)
    )


def swish_gate(gate, up):
    return jax.nn.silu(gate) * up


def local(
    tokens,
    seg_starts,
    norm1_gain,
    w_mix,
    w_gates,
    conv_w,
    decay_rate,
    onorm_gain,
    w_out,
    norm2_gain,
    w_gu,
    w_down,
    cotangent,
):
    f32 = jnp.float32
    bf16 = jnp.bfloat16
    local_rows, width = tokens.shape
    seqs = seg_starts.shape[0]
    heads = w_mix.shape[1]
    mix_cols = w_mix.shape[2]
    value_width = onorm_gain.shape[1]
    hidden = w_down.shape[0]
    mix2d = w_mix.reshape(width, heads * mix_cols)
    gates2d = w_gates.reshape(width, heads * 2)
    out2d = w_out.reshape(heads * value_width, width)
    gu2d = w_gu.reshape(width, 2 * hidden)
    resid = tokens.astype(f32)
    normed1 = rms_norm(resid, norm1_gain).astype(bf16)
    rows1 = lax.all_gather(normed1, "tensor", axis=0, tiled=True)
    total_rows = rows1.shape[0]
    length = total_rows // seqs
    proj = jnp.dot(rows1, mix2d, preferred_element_type=f32).reshape(seqs, length, heads, mix_cols)
    gates_pre = jnp.dot(rows1, gates2d, preferred_element_type=f32).reshape(seqs, length, heads, 2)
    seg, before = jax.vmap(segment_ids, in_axes=(0, None))(seg_starts, length)

    def mixer(p, g, c, r, o):
        return jax.vmap(core, in_axes=(0, 0, None, None, None, 0, 0))(p, g, c, r, o, seg, before)

    heads_out, mixer_back = jax.vjp(mixer, proj, gates_pre, conv_w, decay_rate, onorm_gain)
    mixed = heads_out.astype(bf16).reshape(total_rows, heads * value_width)
    resid2 = resid + lax.psum_scatter(
        jnp.dot(mixed, out2d, preferred_element_type=f32).astype(jnp.bfloat16),
        "tensor",
        scatter_dimension=0,
        tiled=True,
    ).astype(jnp.float32)
    normed2 = rms_norm(resid2, norm2_gain).astype(bf16)
    rows2 = lax.all_gather(normed2, "tensor", axis=0, tiled=True)
    gu = jnp.dot(rows2, gu2d, preferred_element_type=f32).reshape(total_rows, 2, hidden)
    act = swish_gate(gu[:, 0], gu[:, 1]).astype(bf16)
    output = (
        resid2
        + lax.psum_scatter(
            jnp.dot(act, w_down, preferred_element_type=f32).astype(jnp.bfloat16),
            "tensor",
            scatter_dimension=0,
            tiled=True,
        ).astype(jnp.float32)
    ).astype(bf16)
    cot_rows = lax.all_gather(cotangent, "tensor", axis=0, tiled=True)
    grad_down = jnp.dot(act.T, cot_rows, preferred_element_type=f32)
    d_act = jnp.dot(cot_rows, w_down.T, preferred_element_type=f32)
    _, swish_back = jax.vjp(swish_gate, gu[:, 0], gu[:, 1])
    d_gate, d_up = swish_back(d_act)
    d_gu = jnp.stack([d_gate, d_up], axis=1).astype(bf16).reshape(total_rows, 2 * hidden)
    grad_gu = jnp.dot(rows2.T, d_gu, preferred_element_type=f32).reshape(width, 2, hidden)
    d_normed2 = lax.psum_scatter(
        jnp.dot(d_gu, gu2d.T, preferred_element_type=f32).astype(jnp.bfloat16),
        "tensor",
        scatter_dimension=0,
        tiled=True,
    ).astype(jnp.float32)
    _, norm2_back = jax.vjp(rms_norm, resid2, norm2_gain)
    d_resid_ffn, gain2_part = norm2_back(d_normed2)
    d_resid2 = cotangent.astype(f32) + d_resid_ffn
    d_rows = lax.all_gather(d_resid2.astype(bf16), "tensor", axis=0, tiled=True)
    grad_out = jnp.dot(mixed.T, d_rows, preferred_element_type=f32).reshape(
        heads, value_width, width
    )
    d_heads = jnp.dot(d_rows, out2d.T, preferred_element_type=f32).reshape(
        seqs, length, heads, value_width
    )
    d_proj, d_gates_pre, d_conv, d_rate, d_onorm = mixer_back(d_heads)
    d_proj_b = d_proj.astype(bf16).reshape(total_rows, heads * mix_cols)
    d_gates_b = d_gates_pre.astype(bf16).reshape(total_rows, heads * 2)
    grad_mix = jnp.dot(rows1.T, d_proj_b, preferred_element_type=f32).reshape(
        width, heads, mix_cols
    )
    grad_gates = jnp.dot(rows1.T, d_gates_b, preferred_element_type=f32).reshape(width, heads, 2)
    d_normed1 = lax.psum_scatter(
        (
            jnp.dot(d_proj_b, mix2d.T, preferred_element_type=f32)
            + jnp.dot(d_gates_b, gates2d.T, preferred_element_type=f32)
        ).astype(jnp.bfloat16),
        "tensor",
        scatter_dimension=0,
        tiled=True,
    ).astype(jnp.float32)
    _, norm1_back = jax.vjp(rms_norm, resid, norm1_gain)
    d_resid1, gain1_part = norm1_back(d_normed1)
    grad_tokens = (d_resid2 + d_resid1).astype(bf16)
    grad_conv, grad_rate, grad_onorm = lax.psum((d_conv, d_rate, d_onorm), "dp")
    mix_share, gates_share, out_share, gu_share, down_share, gain1_share, gain2_share = (
        lax.psum_scatter(grad_mix, "dp", scatter_dimension=0, tiled=True),
        lax.psum_scatter(grad_gates, "dp", scatter_dimension=0, tiled=True),
        lax.psum_scatter(grad_out, "dp", scatter_dimension=2, tiled=True),
        lax.psum_scatter(grad_gu, "dp", scatter_dimension=0, tiled=True),
        lax.psum_scatter(grad_down, "dp", scatter_dimension=1, tiled=True),
        lax.psum_scatter(gain1_part, "dp", scatter_dimension=0, tiled=True),
        lax.psum_scatter(gain2_part, "dp", scatter_dimension=0, tiled=True),
    )
    gain1_total, gain2_total = lax.psum((gain1_share, gain2_share), "tensor")
    return (
        output,
        grad_tokens,
        gain1_total,
        mix_share,
        gates_share,
        grad_conv,
        grad_rate,
        grad_onorm,
        out_share,
        gain2_total,
        gu_share,
        down_share,
    )


def solution(mesh):
    in_specs = (
        P(("dp", "tensor"), None),
        P("dp", None),
        P(),
        P(None, "tensor", None),
        P(None, "tensor", None),
        P(None, "tensor", None),
        P("tensor"),
        P("tensor", None),
        P("tensor", None, None),
        P(),
        P(None, None, "tensor"),
        P("tensor", None),
        P(("dp", "tensor"), None),
    )
    out_specs = (
        P(("dp", "tensor"), None),
        P(("dp", "tensor"), None),
        P("dp"),
        P("dp", "tensor", None),
        P("dp", "tensor", None),
        P(None, "tensor", None),
        P("tensor"),
        P("tensor", None),
        P("tensor", None, "dp"),
        P("dp"),
        P("dp", None, "tensor"),
        P("tensor", "dp"),
    )
    return jax.shard_map(local, mesh=mesh, in_specs=in_specs, out_specs=out_specs, check_vma=False)
```

profile of v0, /device:TPU:0, one launch (start us, length us, event | category | flops | bytes accessed | tf_op | source)
XLA Modules:
  0.0 1323.5 jit_solution(16078722661583106483)
XLA Ops:
  45.3 309.4 %while.89 = (s32[]{:T(128)}, f32[1,2,128,256]{3,2,1,0:T(8,128)S(1)}, f32[8,1,64,2,256]{4,2,3,1,0:T(8,128)}, pred[8,1,2,64,64]{4,3,2,1,0:T(32,128)(4,1)}, f32[8,1...) while((s32[]{:T(128)}, ...), condition=%wide.region_8.9_spmd.clone.clone.clone, body=%wide.region_6.8_spmd.clone.clone.sunk.clone | while | flops 227423296 | bytes 5225970 | solution.py:92
  53.5 10.5 custom-call.50
  92.1 10.5 custom-call.50
  130.8 10.5 custom-call.50
  169.5 10.5 custom-call.50
  208.2 10.5 custom-call.50
  246.9 10.5 custom-call.50
  285.5 10.5 custom-call.50
  324.3 10.5 custom-call.50
  365.3 24.9 %reduce-scatter.12.cloned.1.call-done = bf16[128,1024]{1,0:T(8,128)(2,1)} async-done(((bf16[512,1024]{1,0:T(8,128)(2,1)}), bf16[128,1024]{1,0:T(8,128)(2,1)}) %reduce-scatter.12.cloned.1.call-update) | async-done | bytes 262160 | tf_op jit(solution)/shard_map/reduce_scatter | solution.py:147
  394.0 16.1 %all-gather.7.cloned.1.call-done = bf16[512,1024]{1,0:T(8,128)(2,1)} async-done(((bf16[128,1024]{1,0:T(8,128)(2,1)}), bf16[512,1024]{1,0:T(8,128)(2,1)}) %all-gather.7.cloned.1.call-update) | async-done | bytes 1048592 | tf_op jit(solution)/shard_map/all_gather | solution.py:154
  414.6 13.6 %all-gather.9.cloned.1.call-done = bf16[512,1024]{1,0:T(8,128)(2,1)} async-done(((bf16[128,1024]{1,0:T(8,128)(2,1)}), bf16[512,1024]{1,0:T(8,128)(2,1)}) %all-gather.9.cloned.1.call-update) | async-done | bytes 1048592 | tf_op jit(solution)/shard_map/all_gather | solution.py:166
  436.1 24.9 %reduce-scatter.16.cloned.1.call-done = bf16[128,1024]{1,0:T(8,128)(2,1)} async-done(((bf16[512,1024]{1,0:T(8,128)(2,1)}), bf16[128,1024]{1,0:T(8,128)(2,1)}) %reduce-scatter.16.cloned.1.call-update) | async-done | bytes 262160 | tf_op jit(solution)/shard_map/reduce_scatter | solution.py:173
  464.4 16.7 %all-gather.11.cloned.1.call-done = bf16[512,1024]{1,0:T(8,128)(2,1)} async-done(((bf16[128,1024]{1,0:T(8,128)(2,1)}), bf16[512,1024]{1,0:T(8,128)(2,1)}) %all-gather.11.cloned.1.call-update) | async-done | bytes 1048592 | tf_op jit(solution)/shard_map/all_gather | solution.py:182
  494.4 307.3 %while.88 = (s32[]{:T(128)}, f32[1,2,128,256]{2,3,1,0:T(8,128)S(1)}, f32[8,1,64,2,128]{4,2,0,3,1:T(8,128)}, f32[8,1,64,2,128]{4,2,0,3,1:T(8,128)}, f32[8,1,64,2,...) while((s32[]{:T(128)}, ...), condition=%wide.region_25.26_spmd.clone.clone, body=%wide.region_16.25_spmd.clone.sunk.clone | while | flops 460795968 | bytes 9110692 | solution.py:92
  728.9 9.8 custom-call.49
  767.3 9.8 custom-call.49
  847.4 30.7 %reduce-scatter.28.cloned.1.call-done = f32[128,4]{1,0:T(8,128)} async-done(((f32[1024,4]{1,0:T(8,128)}), f32[128,4]{1,0:T(8,128)}) %reduce-scatter.28.cloned.1.call-update) | async-done | bytes 2064
  879.7 24.7 %reduce-scatter.18.cloned.1.call-done = bf16[128,1024]{1,0:T(8,128)(2,1)} async-done(((bf16[512,1024]{1,0:T(8,128)(2,1)}), bf16[128,1024]{1,0:T(8,128)(2,1)}) %reduce-scatter.18.cloned.1.call-update) | async-done | bytes 262160 | tf_op jit(solution)/shard_map/reduce_scatter | solution.py:196
  905.6 37.7 %all-reduce.24 = (f32[1024]{0:T(1024)S(1)}, f32[4,2,512]{2,1,0:T(2,128)}, f32[2]{0:T(128)}, f32[2,256]{1,0:T(2,128)}, f32[1024]{0:T(1024)S(1)}) all-reduce(f32[1024]{0:T(1024)S(1)} %get-tuple-element.1960, f32[4,2,512]{2,1,0:T(2,128)S(1)} %pad_add_fusion, f32[2]{0:T(128)S(1)} %neg.95, ...), channel_id=6, replica_groups=mesh['dp'=8,'tensor'=4] {'dp'}, use_global_device_ids=true, to_apply=%region_31.32.clone | all-reduce | flops 6658 | bytes 53264
  952.5 100.8 %reduce-scatter.20.cloned.1.call-done = f32[128,2,768]{2,0,1:T(8,128)} async-done(((f32[1024,2,768]{2,0,1:T(8,128)}), f32[128,2,768]{2,0,1:T(8,128)}) %reduce-scatter.20.cloned.1.call-update) | async-done | bytes 786448 | tf_op jit(solution)/shard_map/reduce_scatter | solution.py:210
  1055.9 73.9 %reduce-scatter.26.cloned.1.call-done = f32[704,128]{1,0:T(8,128)} async-done(((f32[704,1024]{1,0:T(8,128)}), f32[704,128]{1,0:T(8,128)}) %reduce-scatter.26.cloned.1.call-update) | async-done | bytes 360464 | tf_op jit(solution)/shard_map/reduce_scatter | solution.py:214
  1129.8 72.3 %reduce-scatter.22.cloned.1.call-done = f32[2,256,128]{2,1,0:T(8,128)} async-done(((f32[2,256,1024]{2,1,0:T(8,128)}), f32[2,256,128]{2,1,0:T(8,128)}) %reduce-scatter.22.cloned.1.call-update) | async-done | bytes 262160 | tf_op jit(solution)/shard_map/reduce_scatter | solution.py:212
  1202.1 114.3 %reduce-scatter.24.cloned.1.call-done = f32[128,2,704]{0,2,1:T(8,128)} async-done(((f32[1024,2,704]{0,2,1:T(8,128)}), f32[128,2,704]{0,2,1:T(8,128)}) %reduce-scatter.24.cloned.1.call-update) | async-done | bytes 720912 | tf_op jit(solution)/shard_map/reduce_scatter | solution.py:213
  (948 shorter events, 651.7 us)
Async XLA Ops:
  7.2 402.9 %copy-start = (bf16[1024,2,704]{0,2,1:T(8,128)(2,1)S(1)}, bf16[1024,2,704]{0,2,1:T(8,128)(2,1)}, u32[]{:S(2)}) copy-start(bf16[1024,2,704]{0,2,1:T(8,128)(2,1)} %param.27) | copy-start | bytes 8650756
  7.2 22.7 %all-gather.5.cloned.1.call-start = ((), (), s32[]{:S(2)}) async-start(), calls=%async_computation.9 | async-start | bytes 1310720 | tf_op jit(solution)/shard_map/all_gather | solution.py:135
  10.3 379.9 %reduce-scatter.12.cloned.1.call-start = ((), (), s32[]{:S(2)}) async-start(), calls=%async_computation.10 | async-start | bytes 1310720 | tf_op jit(solution)/shard_map/reduce_scatter | solution.py:147
  22.5 22.1 %copy-start.59 = (f32[2]{0:T(128)}, f32[2]{0:T(128)S(1)}, u32[]{:S(2)}) copy-start(f32[2]{0:T(128)S(1)} %neg.88) | copy-start | bytes 28
  362.1 28.2 %copy-start.8 = (bf16[128,1024]{1,0:T(8,128)(2,1)S(1)}, bf16[128,1024]{1,0:T(8,128)(2,1)}, u32[]{:S(2)}) copy-start(bf16[128,1024]{1,0:T(8,128)(2,1)} %param.17) | copy-start | bytes 786436
  362.1 29.3 %copy-start.28 = (f32[1024]{0:T(1024)S(1)}, f32[1024]{0:T(1024)}, u32[]{:S(2)}) copy-start(f32[1024]{0:T(1024)} %param.26) | copy-start | bytes 12292
  365.3 44.8 %all-gather.7.cloned.1.call-start = ((), (), s32[]{:S(2)}) async-start(), calls=%async_computation.11 | async-start | bytes 1310720 | tf_op jit(solution)/shard_map/all_gather | solution.py:154
  393.2 35.0 %all-gather.9.cloned.1.call-start = ((), (), s32[]{:S(2)}) async-start(), calls=%async_computation.13 | async-start | bytes 1310720 | tf_op jit(solution)/shard_map/all_gather | solution.py:166
  393.8 67.3 %reduce-scatter.16.cloned.1.call-start = ((), (), s32[]{:S(2)}) async-start(), calls=%async_computation.14 | async-start | bytes 1310720 | tf_op jit(solution)/shard_map/reduce_scatter | solution.py:173
  433.2 27.8 %copy-start.12 = (bf16[128,1024]{1,0:T(8,128)(2,1)S(1)}, bf16[128,1024]{1,0:T(8,128)(2,1)}, u32[]{:S(2)}) copy-start(bf16[128,1024]{1,0:T(8,128)(2,1)} %reduce-scatter.12.cloned.1.call-done) | copy-start | bytes 786436
  436.0 45.0 %copy-start.63 = (bf16[2,256,1024]{2,1,0:T(8,128)(2,1)S(1)}, bf16[2,256,1024]{2,1,0:T(8,128)(2,1)}, u32[]{:S(2)}) copy-start(bf16[2,256,1024]{2,1,0:T(8,128)(2,1)} %param.25) | copy-start | bytes 3145732
  436.1 45.0 %all-gather.11.cloned.1.call-start = ((), (), s32[]{:S(2)}) async-start(), calls=%async_computation.15 | async-start | bytes 1310720 | tf_op jit(solution)/shard_map/all_gather | solution.py:182
  464.2 413.9 %reduce-scatter.28.cloned.1.call-start = ((), (), s32[]{:S(2)}) async-start(), calls=%async_computation.21 | async-start | bytes 589824
  464.4 21.2 %copy-start.9 = (f32[8,1,64,2,256]{4,2,0,3,1:T(8,128)S(1)}, f32[8,1,64,2,256]{4,2,0,3,1:T(8,128)}, u32[]{:S(2)}) copy-start(f32[8,1,64,2,256]{4,2,0,3,1:T(8,128)} %copy.368) | copy-start | bytes 3145732
  815.3 89.1 %reduce-scatter.18.cloned.1.call-start = ((), (), s32[]{:S(2)}) async-start(), calls=%async_computation.16 | async-start | bytes 1310720 | tf_op jit(solution)/shard_map/reduce_scatter | solution.py:196
  820.9 129.2 %reduce-scatter.14.cloned.1.call-start = ((), (), s32[]{:S(2)}) async-start(), calls=%async_computation.12 | async-start | bytes 1310720 | tf_op jit(solution)/shard_map/reduce_scatter | solution.py:159
  826.6 226.7 %reduce-scatter.20.cloned.1.call-start = ((), (), s32[]{:S(2)}) async-start(), calls=%async_computation.17 | async-start | bytes 7077888 | tf_op jit(solution)/shard_map/reduce_scatter | solution.py:210
  832.6 297.3 %reduce-scatter.26.cloned.1.call-start = ((), (), s32[]{:S(2)}) async-start(), calls=%async_computation.20 | async-start | bytes 3244032 | tf_op jit(solution)/shard_map/reduce_scatter | solution.py:214
  836.3 365.8 %reduce-scatter.22.cloned.1.call-start = ((), (), s32[]{:S(2)}) async-start(), calls=%async_computation.18 | async-start | bytes 2359296 | tf_op jit(solution)/shard_map/reduce_scatter | solution.py:212
  839.8 476.7 %reduce-scatter.24.cloned.1.call-start = ((), (), s32[]{:S(2)}) async-start(), calls=%async_computation.19 | async-start | bytes 6488064 | tf_op jit(solution)/shard_map/reduce_scatter | solution.py:213
  845.2 59.2 %copy-start.31 = (f32[1024]{0:T(1024)S(1)}, f32[1024]{0:T(1024)}, u32[]{:S(2)}) copy-start(f32[1024]{0:T(1024)} %param.19) | copy-start | bytes 12292
  845.2 59.2 %copy-start.58 = (f32[128]{0:T(128)S(1)}, f32[128]{0:T(128)}, u32[]{:S(2)}) copy-start(f32[128]{0:T(128)} %copy-done.57) | copy-start | bytes 1540
  845.2 104.8 %copy-start.62 = (f32[128]{0:T(128)S(1)}, f32[128]{0:T(128)}, u32[]{:S(2)}) copy-start(f32[128]{0:T(128)} %copy-done.61) | copy-start | bytes 1540
  878.1 438.4 %copy-start.1 = (bf16[1024,2,704]{0,2,1:T(8,128)(2,1)S(1)}, bf16[1024,2,704]{0,2,1:T(8,128)(2,1)}, u32[]{:S(2)}) copy-start(bf16[1024,2,704]{0,2,1:T(8,128)(2,1)} %param.27) | copy-start | bytes 8650756
  (88 other events, 384.3 us)
Sparse Core Ops, SparseCore 0:
  10.4 19.4 all-gather.4
  365.4 24.8 reduce-scatter.11
  393.3 16.6 all-gather.6
  411.4 16.6 all-gather.8
  436.2 24.7 reduce-scatter.15
  464.3 16.6 all-gather.10
  815.4 62.6 reduce-scatter.27
  880.6 23.7 reduce-scatter.17
  907.0 24.7 reduce-scatter.13
  935.2 117.9 reduce-scatter.19
  1057.4 72.3 reduce-scatter.25
  1133.8 68.3 reduce-scatter.21
  1206.4 110.0 reduce-scatter.23
where the time goes:
time: 1340 us; the launch traced here: 1320 us
  waiting for transfers between devices  520 us (39%)
  other arithmetic  305 us (23%)
  matrix products  288 us (21%)
  local copies, waits for them, and re-layouts  148 us (11%)
  blocking collectives  44.3 us (3%)
  between operations  16 us (1%)
    another operation x64, other arithmetic, step(): lax.linalg.triangular_solve(unit[None] + lower, rhs, left_side=True, lowe...  171 us
    reduce_scatter x1, waiting for transfers between devices, local(): lax.psum_scatter(grad_gu, 'dp', scatter_dimension=0, tiled=True)  114 us
    reduce_scatter x1, waiting for transfers between devices, local(): lax.psum_scatter(grad_mix, 'dp', scatter_dimension=0, tiled=True)  101 us
    reduce_scatter x1, waiting for transfers between devices, local(): lax.psum_scatter(grad_down, 'dp', scatter_dimension=1, tiled=True)  73.9 us
    reduce_scatter x1, waiting for transfers between devices, local(): lax.psum_scatter(grad_out, 'dp', scatter_dimension=2, tiled=True)  72.3 us
    dynamic_update_slice x40, other arithmetic, core(): _, reads = lax.scan(step, start_state, items)  48.5 us
    unnamed x1, blocking collectives  37.7 us
    dot_general x24, matrix products, step(): jnp.einsum('thd,hde->hte', q_blk, state, precision=highest)  37.5 us
  transfers between devices with their start and end apart: 13, of which 12 were waited for; matrix products, arithmetic and copies ran while one was open for 4% of the time, Pallas kernels for 0%

commit v1 on v0

v1 whole, which is shorter than its diff:
```python
import functools

import jax
import jax.numpy as jnp
from jax import lax
from jax.experimental import pallas as pl
from jax.experimental.pallas import tpu as pltpu
from jax.sharding import PartitionSpec as P

BLOCK = 64
HALO = 8
HI = lax.Precision.HIGHEST


def contract(a, b, dims, exact=False):
    if exact:
        return lax.dot_general(a, b, (dims, ((), ())), precision=HI, preferred_element_type=jnp.float32)
    a, b = a.astype(jnp.bfloat16), b.astype(jnp.bfloat16)
    return lax.dot_general(a, b, (dims, ((), ())), preferred_element_type=jnp.float32)


NN, NT, TN = ((1,), (0,)), ((1,), (1,)), ((0,), (0,))


@functools.partial(jax.custom_vjp, nondiff_argnums=(2,))
def mm_nn(a, b, exact=False):
    return contract(a, b, NN, exact)


mm_nn.defvjp(
    lambda a, b, exact: (contract(a, b, NN, exact), (a, b)),
    lambda exact, res, g: (contract(g, res[1], NT, exact), contract(res[0], g, TN, exact)),
)


@functools.partial(jax.custom_vjp, nondiff_argnums=(2,))
def mm_nt(a, b, exact=False):
    return contract(a, b, NT, exact)


mm_nt.defvjp(
    lambda a, b, exact: (contract(a, b, NT, exact), (a, b)),
    lambda exact, res, g: (contract(g, res[1], NN, exact), contract(g, res[0], TN, exact)),
)


@functools.partial(jax.custom_vjp, nondiff_argnums=(2,))
def mm_tn(a, b, exact=False):
    return contract(a, b, TN, exact)


mm_tn.defvjp(
    lambda a, b, exact: (contract(a, b, TN, exact), (a, b)),
    lambda exact, res, g: (contract(res[1], g, NT, exact), contract(res[0], g, NN, exact)),
)


@jax.custom_vjp
def solve(lower, rhs, inverse):
    return contract(inverse, rhs, NN)


def solve_fwd(lower, rhs, inverse):
    errs = contract(inverse, rhs, NN)
    return errs, (inverse, errs)


def solve_bwd(res, g):
    inverse, errs = res
    d_rhs = contract(inverse, g, TN)
    return -contract(d_rhs, errs, NT), d_rhs, jnp.zeros_like(inverse)


solve.defvjp(solve_fwd, solve_bwd)


@functools.partial(jax.custom_vjp, nondiff_argnums=(1,))
def keepsum(x, axis):
    return jnp.sum(x, axis=axis, keepdims=True)


keepsum.defvjp(
    lambda x, axis: (jnp.sum(x, axis=axis, keepdims=True), x),
    lambda axis, x, g: (jnp.broadcast_to(g, x.shape),),
)


@functools.partial(jax.custom_vjp, nondiff_argnums=(1,))
def spread(x, shape):
    return jnp.broadcast_to(x, shape)


def spread_bwd(shape, x, g):
    for axis in range(2):
        if x.shape[axis] == 1 and shape[axis] != 1:
            g = jnp.sum(g, axis=axis, keepdims=True)
    return (g,)


spread.defvjp(lambda x, shape: (jnp.broadcast_to(x, shape), x), spread_bwd)


@functools.partial(jax.custom_vjp, nondiff_argnums=(1,))
def lagged(ext, lag):
    return pltpu.roll(ext, lag, 0)[HALO:] if lag else ext[HALO:]


def lagged_bwd(lag, ext, g):
    full = jnp.concatenate([jnp.zeros((HALO, g.shape[1]), g.dtype), g], axis=0)
    return (pltpu.roll(full, full.shape[0] - lag, 0) if lag else full,)


lagged.defvjp(lambda ext, lag: (lagged(ext, lag), ext), lagged_bwd)


@jax.custom_vjp
def softplus(x):
    return jnp.maximum(x, 0.0) + jnp.log1p(jnp.exp(-jnp.abs(x)))


softplus.defvjp(lambda x: (softplus(x), x), lambda x, g: (g * jax.nn.sigmoid(x),))


def silu(x):
    return x * jax.nn.sigmoid(x)


def rms_norm(rows, gain):
    return rows * lax.rsqrt(jnp.mean(rows * rows, axis=-1, keepdims=True) + 1e-06) * gain


def segment_ids(starts_row, length):
    places = jnp.arange(length, dtype=jnp.int32)
    flags = jnp.any(starts_row[:, None] == places[None, :], axis=0).astype(jnp.int32)
    seg = jnp.cumsum(flags)
    before = jnp.concatenate([seg[:1], seg[:-1]])
    columns = [seg]
    for lag in range(1, 4):
        moved = jnp.pad(seg, (lag, 0), constant_values=-1)[:length]
        columns.append(moved == seg)
    columns.append(seg == jnp.repeat(before[::BLOCK], BLOCK))
    columns += [jnp.zeros_like(seg)] * 3
    return jnp.stack([c.astype(jnp.float32) for c in columns], axis=1)


def masks():
    shape = (BLOCK, BLOCK)
    row = lax.broadcasted_iota(jnp.int32, shape, 0)
    col = lax.broadcasted_iota(jnp.int32, shape, 1)
    return row, col


def unit_inverse(lowers):
    row, col = masks()
    out = None
    size = 0
    while (1 << size) < BLOCK:
        part = jnp.logical_and(
            (row >> (size + 1)) == (col >> (size + 1)),
            jnp.logical_and(((row >> size) & 1) == 1, ((col >> size) & 1) == 0),
        )
        cut = [jnp.where(part, low, 0.0) for low in lowers]
        if out is None:
            unit = (row == col).astype(jnp.float32)
            out = [unit - c for c in cut]
        else:
            mid = [contract(c, t, NN, True) for c, t in zip(cut, out)]
            out = [t - contract(t, m, NN, True) for t, m in zip(out, mid)]
        size += 1
    return out


def front(ext, alpha_pre, beta_pre, taps, rate, aux, key_width):
    rows = BLOCK
    wide = (rows, ext.shape[1])
    square = (BLOCK, BLOCK)
    total = spread(taps[3], wide) * lagged(ext, 0)
    for lag in range(1, 4):
        keep = jnp.broadcast_to(aux[lag], wide)
        total = total + spread(taps[3 - lag], wide) * (lagged(ext, lag) * keep)
    act = silu(total)

    def unit_rows(x):
        return x * spread(lax.rsqrt(keepsum(x * x, 1) + 1e-06), x.shape)

    return act, unit_rows


def block_terms(query, keys, beta_pre, alpha_pre, rate, aux):
    square = (BLOCK, BLOCK)
    row, col = masks()
    eye = (row == col).astype(jnp.float32)
    seg_col = jnp.broadcast_to(aux[0], square)
    seg_row = jnp.broadcast_to(jnp.sum(eye * seg_col, axis=0, keepdims=True), square)
    live = jnp.logical_and(seg_col == seg_row, row >= col)
    beta = jax.nn.sigmoid(beta_pre)
    logd = -spread(rate, alpha_pre.shape) * softplus(alpha_pre)
    incl = (row >= col).astype(jnp.float32)
    logd_row = keepsum(eye * spread(logd, square), 0)
    cum = keepsum(incl * spread(logd_row, square), 1)
    cum_row = keepsum(eye * spread(cum, square), 0)
    diff = spread(cum, square) - spread(cum_row, square)
    within = jnp.where(live, jnp.exp(jnp.where(live, diff, 0.0)), 0.0)
    carried = jnp.exp(cum) * aux[4]
    kk = mm_nt(keys, keys, True)
    strict = (row > col).astype(jnp.float32)
    lower = spread(beta, square) * within * kk * strict
    place = lax.broadcasted_iota(jnp.int32, (BLOCK, 1), 0)
    last = (place == BLOCK - 1).astype(jnp.float32)
    cum_last = spread(keepsum(cum * last, 0), cum.shape)
    seg_last = jnp.broadcast_to(jnp.sum(aux[0] * last, axis=0, keepdims=True), cum.shape)
    same = seg_last == aux[0]
    final = jnp.where(same, jnp.exp(jnp.where(same, cum_last - cum, 0.0)), 0.0)
    carried_last = keepsum(carried * last, 0)
    return beta, within, carried, lower, final, carried_last


def split_heads(ext, taps, aux, key_width):
    act, unit_rows = front(ext, None, None, taps, None, aux, key_width)
    query = unit_rows(act[:, :key_width]) * key_width ** (-0.5)
    keys = unit_rows(act[:, key_width : 2 * key_width])
    return query, keys, act[:, 2 * key_width :]


def advance(query, keys, values, terms, state, inverse, gate_out, onorm):
    beta, within, carried, lower, final, carried_last = terms
    tall = values.shape
    rhs = spread(beta, tall) * (values - spread(carried, tall) * mm_nn(keys, state))
    errs = solve(lower, rhs, inverse)
    read = spread(carried, tall) * mm_nn(query, state)
    read = read + mm_nn(within * mm_nt(query, keys), errs)
    new_state = spread(carried_last, state.shape) * state
    new_state = new_state + mm_tn(spread(final, keys.shape) * keys, errs)
    scale = lax.rsqrt(keepsum(read * read, 1) * (1.0 / tall[1]) + 1e-05)
    out = read * spread(scale, tall) * spread(onorm, tall) * silu(gate_out)
    return out, new_state


def head_inputs(h, dims, halo_ref, proj_ref, gates_ref, conv_ref, rate_ref, onorm_ref):
    heads, mix, conv, value = dims
    base = h * mix
    ext = jnp.concatenate(
        [halo_ref[:, base : base + conv], proj_ref[:, base : base + conv]], axis=0
    )
    gate_out = proj_ref[:, base + conv : base + mix]
    alpha_pre = gates_ref[:, 2 * h : 2 * h + 1]
    beta_pre = gates_ref[:, 2 * h + 1 : 2 * h + 2]
    taps = tuple(conv_ref[i : i + 1, h * conv : (h + 1) * conv] for i in range(4))
    rate = rate_ref[:, h : h + 1]
    onorm = onorm_ref[h : h + 1, :]
    return ext, gate_out, alpha_pre, beta_pre, taps, rate, onorm


def forward_kernel(dims, halo_ref, proj_ref, gates_ref, aux_ref, conv_ref, rate_ref, onorm_ref,
                   out_ref, states_ref, inv_ref, state):
    heads, mix, conv, value = dims
    key_width = (conv - value) // 2

    @pl.when(pl.program_id(1) == 0)
    def _():
        state[...] = jnp.zeros_like(state)

    aux = [aux_ref[:, i : i + 1] for i in range(5)]
    work = []
    for h in range(heads):
        ext, gate_out, alpha_pre, beta_pre, taps, rate, onorm = head_inputs(
            h, dims, halo_ref, proj_ref, gates_ref, conv_ref, rate_ref, onorm_ref
        )
        query, keys, values = split_heads(ext, taps, aux, key_width)
        terms = block_terms(query, keys, beta_pre, alpha_pre, rate, aux)
        work.append((query, keys, values, terms, gate_out, onorm))
    inverses = unit_inverse([w[3][3] for w in work])
    for h in range(heads):
        query, keys, values, terms, gate_out, onorm = work[h]
        old = state[h * key_width : (h + 1) * key_width, :]
        out, new = advance(query, keys, values, terms, old, inverses[h], gate_out, onorm)
        states_ref[0, h * key_width : (h + 1) * key_width, :] = old
        state[h * key_width : (h + 1) * key_width, :] = new
        inv_ref[0, h * BLOCK : (h + 1) * BLOCK, :] = inverses[h]
        out_ref[:, h * value : (h + 1) * value] = out.astype(out_ref.dtype)


def backward_kernel(dims, halo_ref, proj_ref, gates_ref, aux_ref, conv_ref, rate_ref, onorm_ref,
                    states_ref, inv_ref, d_out_ref,
                    d_proj_ref, d_gates_ref, d_conv_ref, d_rate_ref, d_onorm_ref, d_state, spill):
    heads, mix, conv, value = dims
    key_width = (conv - value) // 2

    @pl.when(pl.program_id(1) == 0)
    def _():
        d_state[...] = jnp.zeros_like(d_state)
        spill[...] = jnp.zeros_like(spill)

    @pl.when(jnp.logical_and(pl.program_id(0) == 0, pl.program_id(1) == 0))
    def _():
        d_conv_ref[...] = jnp.zeros_like(d_conv_ref)
        d_rate_ref[...] = jnp.zeros_like(d_rate_ref)
        d_onorm_ref[...] = jnp.zeros_like(d_onorm_ref)

    aux = [aux_ref[:, i : i + 1] for i in range(5)]
    lane = lax.broadcasted_iota(jnp.int32, (BLOCK, 2 * heads), 1)
    d_gates = jnp.zeros((BLOCK, 2 * heads), jnp.float32)
    for h in range(heads):
        ext, gate_out, alpha_pre, beta_pre, taps, rate, onorm = head_inputs(
            h, dims, halo_ref, proj_ref, gates_ref, conv_ref, rate_ref, onorm_ref
        )
        old = states_ref[0, h * key_width : (h + 1) * key_width, :]
        inverse = inv_ref[0, h * BLOCK : (h + 1) * BLOCK, :]

        act, act_back = jax.vjp(
            lambda e, t: front(e, None, None, t, None, aux, key_width)[0], ext, taps
        )
        raw_q = act[:, :key_width]
        raw_k = act[:, key_width : 2 * key_width]
        values = act[:, 2 * key_width :]

        def rest(raw_q, raw_k, values, gate_out, alpha_pre, beta_pre, rate, onorm, old):
            def unit_rows(x):
                return x * spread(lax.rsqrt(keepsum(x * x, 1) + 1e-06), x.shape)

            query = unit_rows(raw_q) * key_width ** (-0.5)
            keys = unit_rows(raw_k)
            terms = block_terms(query, keys, beta_pre, alpha_pre, rate, aux)
            return advance(query, keys, values, terms, old, inverse, gate_out, onorm)

        _, back = jax.vjp(
            rest, raw_q, raw_k, values, gate_out, alpha_pre, beta_pre, rate, onorm, old
        )
        d_out = d_out_ref[:, h * value : (h + 1) * value]
        span = slice(h * key_width, (h + 1) * key_width)
        d_q, d_k, d_v, d_gate, d_alpha, d_beta, d_rate, d_onorm, d_old = back(
            (d_out, d_state[span, :])
        )
        d_state[span, :] = d_old
        d_ext, d_taps = act_back(jnp.concatenate([d_q, d_k, d_v], axis=1))
        cols = slice(h * conv, (h + 1) * conv)
        carry = jnp.concatenate(
            [jnp.zeros((BLOCK - HALO, conv), jnp.float32), spill[:, cols]], axis=0
        )
        d_mixed = d_ext[HALO:] + carry
        spill[:, cols] = d_ext[:HALO]
        base = h * mix
        d_proj_ref[:, base : base + conv] = d_mixed.astype(d_proj_ref.dtype)
        d_proj_ref[:, base + conv : base + mix] = d_gate.astype(d_proj_ref.dtype)
        for i in range(4):
            d_conv_ref[i : i + 1, cols] += d_taps[i]
        d_rate_ref[h : h + 1, :] += jnp.broadcast_to(d_rate, (1, 128))
        d_onorm_ref[h : h + 1, :] += d_onorm
        d_gates = d_gates + jnp.where(lane == 2 * h, jnp.broadcast_to(d_alpha, lane.shape), 0.0)
        d_gates = d_gates + jnp.where(lane == 2 * h + 1, jnp.broadcast_to(d_beta, lane.shape), 0.0)
    d_gates_ref[...] = d_gates.astype(d_gates_ref.dtype)


def common_specs(dims, blocks, order):
    heads, mix, conv, value = dims
    ratio = BLOCK // HALO
    at = lambda s, b: s * blocks + order(b)
    return [
        pl.BlockSpec((HALO, heads * mix), lambda s, b: (jnp.maximum(at(s, b) * ratio - 1, 0), 0)),
        pl.BlockSpec((BLOCK, heads * mix), lambda s, b: (at(s, b), 0)),
        pl.BlockSpec((BLOCK, heads * 2), lambda s, b: (at(s, b), 0)),
        pl.BlockSpec((BLOCK, 8), lambda s, b: (at(s, b), 0)),
        pl.BlockSpec((4, heads * conv), lambda s, b: (0, 0)),
        pl.BlockSpec((1, heads), lambda s, b: (0, 0)),
        pl.BlockSpec((heads, value), lambda s, b: (0, 0)),
    ], at


def mixer_forward(proj, gates_pre, aux, conv2d, rate, onorm, dims, seqs, interpret=False):
    heads, mix, conv, value = dims
    key_width = (conv - value) // 2
    rows = proj.shape[0]
    blocks = rows // seqs // BLOCK
    specs, at = common_specs(dims, blocks, lambda b: b)
    return pl.pallas_call(
        functools.partial(forward_kernel, dims),
        grid=(seqs, blocks),
        in_specs=specs,
        out_specs=[
            pl.BlockSpec((BLOCK, heads * value), lambda s, b: (at(s, b), 0)),
            pl.BlockSpec((1, heads * key_width, value), lambda s, b: (at(s, b), 0, 0)),
            pl.BlockSpec((1, heads * BLOCK, BLOCK), lambda s, b: (at(s, b), 0, 0)),
        ],
        out_shape=[
            jax.ShapeDtypeStruct((rows, heads * value), jnp.bfloat16),
            jax.ShapeDtypeStruct((seqs * blocks, heads * key_width, value), jnp.float32),
            jax.ShapeDtypeStruct((seqs * blocks, heads * BLOCK, BLOCK), jnp.float32),
        ],
        scratch_shapes=[pltpu.VMEM((heads * key_width, value), jnp.float32)],
        cost_estimate=pl.CostEstimate(flops=rows * heads * 2000000, bytes_accessed=rows * heads * 8192, transcendentals=0),
        name="mixer_forward",
        interpret=interpret,
    )(proj, proj, gates_pre, aux, conv2d, rate, onorm)


def mixer_backward(proj, gates_pre, aux, conv2d, rate, onorm, states, inverses, d_heads, dims, seqs, interpret=False):
    heads, mix, conv, value = dims
    key_width = (conv - value) // 2
    rows = proj.shape[0]
    blocks = rows // seqs // BLOCK
    specs, at = common_specs(dims, blocks, lambda b: blocks - 1 - b)
    return pl.pallas_call(
        functools.partial(backward_kernel, dims),
        grid=(seqs, blocks),
        in_specs=specs + [
            pl.BlockSpec((1, heads * key_width, value), lambda s, b: (at(s, b), 0, 0)),
            pl.BlockSpec((1, heads * BLOCK, BLOCK), lambda s, b: (at(s, b), 0, 0)),
            pl.BlockSpec((BLOCK, heads * value), lambda s, b: (at(s, b), 0)),
        ],
        out_specs=[
            pl.BlockSpec((BLOCK, heads * mix), lambda s, b: (at(s, b), 0)),
            pl.BlockSpec((BLOCK, heads * 2), lambda s, b: (at(s, b), 0)),
            pl.BlockSpec((4, heads * conv), lambda s, b: (0, 0)),
            pl.BlockSpec((heads, 128), lambda s, b: (0, 0)),
            pl.BlockSpec((heads, value), lambda s, b: (0, 0)),
        ],
        out_shape=[
            jax.ShapeDtypeStruct((rows, heads * mix), jnp.bfloat16),
            jax.ShapeDtypeStruct((rows, heads * 2), jnp.bfloat16),
            jax.ShapeDtypeStruct((4, heads * conv), jnp.float32),
            jax.ShapeDtypeStruct((heads, 128), jnp.float32),
            jax.ShapeDtypeStruct((heads, value), jnp.float32),
        ],
        scratch_shapes=[
            pltpu.VMEM((heads * key_width, value), jnp.float32),
            pltpu.VMEM((HALO, heads * conv), jnp.float32),
        ],
        cost_estimate=pl.CostEstimate(flops=rows * heads * 5000000, bytes_accessed=rows * heads * 12288, transcendentals=0),
        name="mixer_backward",
        interpret=interpret,
    )(proj, proj, gates_pre, aux, conv2d, rate, onorm, states, inverses, d_heads)


def swish_gate(gate, up):
    return jax.nn.silu(gate) * up


def local(
    tokens,
    seg_starts,
    norm1_gain,
    w_mix,
    w_gates,
    conv_w,
    decay_rate,
    onorm_gain,
    w_out,
    norm2_gain,
    w_gu,
    w_down,
    cotangent,
):
    f32 = jnp.float32
    bf16 = jnp.bfloat16
    local_rows, width = tokens.shape
    seqs = seg_starts.shape[0]
    heads = w_mix.shape[1]
    mix_cols = w_mix.shape[2]
    value_width = onorm_gain.shape[1]
    hidden = w_down.shape[0]
    mix2d = w_mix.reshape(width, heads * mix_cols)
    gates2d = w_gates.reshape(width, heads * 2)
    out2d = w_out.reshape(heads * value_width, width)
    gu2d = w_gu.reshape(width, 2 * hidden)
    resid = tokens.astype(f32)
    normed1 = rms_norm(resid, norm1_gain).astype(bf16)
    rows1 = lax.all_gather(normed1, "tensor", axis=0, tiled=True)
    total_rows = rows1.shape[0]
    length = total_rows // seqs
    dims = (heads, mix_cols, conv_w.shape[2], value_width)
    proj = jnp.dot(rows1, mix2d, preferred_element_type=f32)
    gates_pre = jnp.dot(rows1, gates2d, preferred_element_type=f32)
    aux = jax.vmap(segment_ids, in_axes=(0, None))(seg_starts, length).reshape(total_rows, 8)
    mixer_args = (proj, gates_pre, aux, conv_w.reshape(4, -1), decay_rate[None, :], onorm_gain)
    mixed, states, inverses = mixer_forward(*mixer_args, dims, seqs)
    resid2 = resid + lax.psum_scatter(
        jnp.dot(mixed, out2d, preferred_element_type=f32).astype(jnp.bfloat16),
        "tensor",
        scatter_dimension=0,
        tiled=True,
    ).astype(jnp.float32)
    normed2 = rms_norm(resid2, norm2_gain).astype(bf16)
    rows2 = lax.all_gather(normed2, "tensor", axis=0, tiled=True)
    gu = jnp.dot(rows2, gu2d, preferred_element_type=f32).reshape(total_rows, 2, hidden)
    act = swish_gate(gu[:, 0], gu[:, 1]).astype(bf16)
    output = (
        resid2
        + lax.psum_scatter(
            jnp.dot(act, w_down, preferred_element_type=f32).astype(jnp.bfloat16),
            "tensor",
            scatter_dimension=0,
            tiled=True,
        ).astype(jnp.float32)
    ).astype(bf16)
    cot_rows = lax.all_gather(cotangent, "tensor", axis=0, tiled=True)
    grad_down = jnp.dot(act.T, cot_rows, preferred_element_type=f32)
    d_act = jnp.dot(cot_rows, w_down.T, preferred_element_type=f32)
    _, swish_back = jax.vjp(swish_gate, gu[:, 0], gu[:, 1])
    d_gate, d_up = swish_back(d_act)
    d_gu = jnp.stack([d_gate, d_up], axis=1).astype(bf16).reshape(total_rows, 2 * hidden)
    grad_gu = jnp.dot(rows2.T, d_gu, preferred_element_type=f32).reshape(width, 2, hidden)
    d_normed2 = lax.psum_scatter(
        jnp.dot(d_gu, gu2d.T, preferred_element_type=f32).astype(jnp.bfloat16),
        "tensor",
        scatter_dimension=0,
        tiled=True,
    ).astype(jnp.float32)
    _, norm2_back = jax.vjp(rms_norm, resid2, norm2_gain)
    d_resid_ffn, gain2_part = norm2_back(d_normed2)
    d_resid2 = cotangent.astype(f32) + d_resid_ffn
    d_rows = lax.all_gather(d_resid2.astype(bf16), "tensor", axis=0, tiled=True)
    grad_out = jnp.dot(mixed.T, d_rows, preferred_element_type=f32).reshape(
        heads, value_width, width
    )
    d_heads = jnp.dot(d_rows, out2d.T, preferred_element_type=f32)
    d_proj_b, d_gates_b, d_conv, d_rate, d_onorm = mixer_backward(
        *mixer_args, states, inverses, d_heads, dims, seqs
    )
    d_conv = d_conv.reshape(conv_w.shape)
    d_rate = d_rate[:, 0]
    grad_mix = jnp.dot(rows1.T, d_proj_b, preferred_element_type=f32)
    grad_gates = jnp.dot(rows1.T, d_gates_b, preferred_element_type=f32).reshape(width, heads, 2)
    d_normed1 = lax.psum_scatter(
        (
            jnp.dot(d_proj_b, mix2d.T, preferred_element_type=f32)
            + jnp.dot(d_gates_b, gates2d.T, preferred_element_type=f32)
        ).astype(jnp.bfloat16),
        "tensor",
        scatter_dimension=0,
        tiled=True,
    ).astype(jnp.float32)
    _, norm1_back = jax.vjp(rms_norm, resid, norm1_gain)
    d_resid1, gain1_part = norm1_back(d_normed1)
    grad_tokens = (d_resid2 + d_resid1).astype(bf16)
    grad_conv, grad_rate, grad_onorm = lax.psum((d_conv, d_rate, d_onorm), "dp")
    mix_share, gates_share, out_share, gu_share, down_share, gain1_share, gain2_share = (
        lax.psum_scatter(grad_mix.astype(bf16), "dp", scatter_dimension=0, tiled=True),
        lax.psum_scatter(grad_gates, "dp", scatter_dimension=0, tiled=True),
        lax.psum_scatter(grad_out.astype(bf16), "dp", scatter_dimension=2, tiled=True),
        lax.psum_scatter(grad_gu.astype(bf16), "dp", scatter_dimension=0, tiled=True),
        lax.psum_scatter(grad_down.astype(bf16), "dp", scatter_dimension=1, tiled=True),
        lax.psum_scatter(gain1_part, "dp", scatter_dimension=0, tiled=True),
        lax.psum_scatter(gain2_part, "dp", scatter_dimension=0, tiled=True),
    )
    mix_share = mix_share.reshape(-1, heads, mix_cols)
    mix_share, out_share, gu_share, down_share = (
        share.astype(f32) for share in (mix_share, out_share, gu_share, down_share)
    )
    gain1_total, gain2_total = lax.psum((gain1_share, gain2_share), "tensor")
    return (
        output,
        grad_tokens,
        gain1_total,
        mix_share,
        gates_share,
        grad_conv,
        grad_rate,
        grad_onorm,
        out_share,
        gain2_total,
        gu_share,
        down_share,
    )


def solution(mesh):
    in_specs = (
        P(("dp", "tensor"), None),
        P("dp", None),
        P(),
        P(None, "tensor", None),
        P(None, "tensor", None),
        P(None, "tensor", None),
        P("tensor"),
        P("tensor", None),
        P("tensor", None, None),
        P(),
        P(None, None, "tensor"),
        P("tensor", None),
        P(("dp", "tensor"), None),
    )
    out_specs = (
        P(("dp", "tensor"), None),
        P(("dp", "tensor"), None),
        P("dp"),
        P("dp", "tensor", None),
        P("dp", "tensor", None),
        P(None, "tensor", None),
        P("tensor"),
        P("tensor", None),
        P("tensor", None, "dp"),
        P("dp"),
        P("dp", None, "tensor"),
        P("tensor", "dp"),
    )
    return jax.shard_map(local, mesh=mesh, in_specs=in_specs, out_specs=out_specs, check_vma=False)
```

time: 1340 us -> 599 us (0.45); the launches traced: 1320 us -> 598 us
  other arithmetic: 305 us -> 22.6 us
  matrix products: 288 us -> 52.9 us
  waiting for transfers between devices: 520 us -> 373 us
  local copies, waits for them, and re-layouts: 148 us -> 37.4 us
  Pallas kernels: 0 us -> 51.8 us
    reduce_scatter x4 -> x1, waiting for transfers between devices: 361 us -> 53.3 us  [local(): lax.psum_scatter(grad_mix.astype(bf16), 'dp', scatter_dimension=0, tiled=...]
    dot_general x157 -> x4, matrix products: 224 us -> 16.6 us  [the longest x1 5.71 us: local(): proj = jnp.dot(rows1, mix2d, preferred_element_type=f32)]
    another operation x117 -> x4, other arithmetic: 182 us -> 0.58 us  [the longest x64 171 us: step(): lax.linalg.triangular_solve(unit[None] + lower, rhs, left_side=True, lowe...]
    unnamed x14 -> x17, waiting for transfers between devices: 31.4 us -> 198 us
    pallas_call x0 -> x2, Pallas kernels: none -> 51.8 us  [the longest x1 26.9 us: mixer_backward(): pl.pallas_call(functools.partial(backward_kernel, dims), grid=(seqs, bloc...]
    dynamic_update_slice x40 -> x0, other arithmetic: 48.5 us -> none  [core(): _, reads = lax.scan(step, start_state, items)]
    dynamic_update_slice x48 -> x0, local copies, waits for them, and re-layouts: 34.1 us -> none  [core(): _, reads = lax.scan(step, start_state, items)]
    another operation x24 -> x0, matrix products: 32.6 us -> none  [step(): lax.linalg.triangular_solve(unit[None] + lower, rhs, left_side=True, lowe...]
  transfers between devices with their start and end apart: 13 -> 13, of which waited for: 12 -> 12; matrix products, arithmetic and copies ran while one was open for 4% -> 14% of each run, Pallas kernels for 0% -> 4%
where the time goes in v1:
time: 599 us; the launch traced here: 598 us
  waiting for transfers between devices  373 us (62%)
  matrix products  52.9 us (9%)
  Pallas kernels  51.8 us (9%)
  blocking collectives  44.8 us (7%)
  local copies, waits for them, and re-layouts  37.4 us (6%)
  other arithmetic  22.6 us (4%)
  between operations  14.8 us (2%)
    unnamed x17, waiting for transfers between devices  198 us
    reduce_scatter x1, waiting for transfers between devices, local(): lax.psum_scatter(grad_mix.astype(bf16), 'dp', scatter_dimension=0, tiled=...  53.3 us
    unnamed x1, blocking collectives  38.4 us
    unnamed x48, local copies, waits for them, and re-layouts  31.2 us
    pallas_call x1, Pallas kernels, mixer_backward(): pl.pallas_call(functools.partial(backward_kernel, dims), grid=(seqs, bloc...  26.9 us
    reduce_scatter x1, waiting for transfers between devices, local(): lax.psum_scatter(jnp.dot(mixed, out2d, preferred_element_type=f32).astype...  24.9 us
    reduce_scatter x1, waiting for transfers between devices, local(): lax.psum_scatter(jnp.dot(d_gu, gu2d.T, preferred_element_type=f32).astype...  24.9 us
    pallas_call x1, Pallas kernels, mixer_forward(): pl.pallas_call(functools.partial(forward_kernel, dims), grid=(seqs, block...  24.9 us
  transfers between devices with their start and end apart: 13, of which 12 were waited for; matrix products, arithmetic and copies ran while one was open for 14% of the time, Pallas kernels for 4%

profile of v1, /device:TPU:0, one launch (start us, length us, event | category | flops | bytes accessed | tf_op | source)
XLA Modules:
  0.0 597.9 jit_solution(1673317157928519283)
XLA Ops:
  16.4 4.1 copy.54
  20.6 9.4 %all-gather.5.cloned.1.call-done = bf16[512,1024]{1,0:T(8,128)(2,1)} async-done(((bf16[128,1024]{1,0:T(8,128)(2,1)}), bf16[512,1024]{1,0:T(8,128)(2,1)}) %all-gather.5.cloned.1.call-update) | async-done | bytes 1048592 | tf_op jit(solution)/shard_map/all_gather | solution.py:467
  32.3 5.7 fusion.31.halo_ref.proj_ref
  38.0 24.9 %mixer_forward.1 = (bf16[512,512]{1,0:T(8,128)(2,1)}, f32[8,256,256]{2,1,0:T(8,128)}, f32[8,128,64]{2,1,0:T(8,128)}) custom-call(f32[512,1536]{1,0:T(8,128)} %fusion.31.halo_ref.proj_ref, f32[512,1536]{1,0:T(8,128)} %fusion.31.halo_ref.proj_ref, f32[512,4]{1,0:T(8,128)} %fusion.32.gates_ref, f32[512,8]{1,0:T(8,128)} %bitcast.116, f32[4,1024]{1,0:T(4,128)} %bitcast.127, ...), custom_call_target="tpu_custom_call" | custom-call | flops 2048000000 | bytes 8388608 | tf_op jit(solution)/shard_map/mixer_forward/pallas_call | solution.py:375
  66.1 24.9 %reduce-scatter.18.cloned.1.call-done = bf16[128,1024]{1,0:T(8,128)(2,1)} async-done(((bf16[512,1024]{1,0:T(8,128)(2,1)}), bf16[128,1024]{1,0:T(8,128)(2,1)}) %reduce-scatter.18.cloned.1.call-update) | async-done | bytes 262160 | tf_op jit(solution)/shard_map/reduce_scatter | solution.py:476
  94.6 16.2 %all-gather.7.cloned.1.call-done = bf16[512,1024]{1,0:T(8,128)(2,1)} async-done(((bf16[128,1024]{1,0:T(8,128)(2,1)}), bf16[512,1024]{1,0:T(8,128)(2,1)}) %all-gather.7.cloned.1.call-update) | async-done | bytes 1048592 | tf_op jit(solution)/shard_map/all_gather | solution.py:483
  110.8 4.6 fusion
  115.4 13.6 %all-gather.9.cloned.1.call-done = bf16[512,1024]{1,0:T(8,128)(2,1)} async-done(((bf16[128,1024]{1,0:T(8,128)(2,1)}), bf16[512,1024]{1,0:T(8,128)(2,1)}) %all-gather.9.cloned.1.call-update) | async-done | bytes 1048592 | tf_op jit(solution)/shard_map/all_gather | solution.py:495
  128.9 3.9 fusion.4
  136.9 24.9 %reduce-scatter.22.cloned.1.call-done = bf16[128,1024]{1,0:T(8,128)(2,1)} async-done(((bf16[512,1024]{1,0:T(8,128)(2,1)}), bf16[128,1024]{1,0:T(8,128)(2,1)}) %reduce-scatter.22.cloned.1.call-update) | async-done | bytes 262160 | tf_op jit(solution)/shard_map/reduce_scatter | solution.py:502
  173.1 8.7 %all-gather.11.cloned.1.call-done = bf16[512,1024]{1,0:T(8,128)(2,1)} async-done(((bf16[128,1024]{1,0:T(8,128)(2,1)}), bf16[512,1024]{1,0:T(8,128)(2,1)}) %all-gather.11.cloned.1.call-update) | async-done | bytes 1048592 | tf_op jit(solution)/shard_map/all_gather | solution.py:511
  185.2 26.9 %mixer_backward.1 = (bf16[512,1536]{1,0:T(8,128)(2,1)}, bf16[512,4]{1,0:T(8,128)(2,1)}, f32[4,1024]{1,0:T(4,128)}, f32[2,128]{1,0:T(2,128)}, f32[2,256]{1,0:T(2,128)}) custom-call(f32[512,1536]{1,0:T(8,128)} %fusion.31.halo_ref.proj_ref, f32[512,1536]{1,0:T(8,128)} %fusion.31.halo_ref.proj_ref, f32[512,4]{1,0:T(8,128)} %fusion.32.gates_ref, ...), custom_call_target="tpu_custom_call" | custom-call | flops 5120000000 | bytes 12582912 | tf_op jit(solution)/shard_map/mixer_backward/pallas_call | solution.py:402
  214.7 5.0 convolution_convert_fusion.1
  219.6 4.6 copy.52
  227.4 3.7 copy.44
  233.6 4.2 fusion.34
  243.2 5.2 convolution_convert_fusion
  255.6 60.1 %reduce-scatter.28.cloned.1.call-done = f32[128,4]{1,0:T(8,128)} async-done(((f32[1024,4]{1,0:T(8,128)}), f32[128,4]{1,0:T(8,128)}) %reduce-scatter.28.cloned.1.call-update) | async-done | bytes 2064
  317.3 73.4 %reduce-scatter.32.cloned.1.call-done = bf16[128,1408]{1,0:T(8,128)(2,1)} async-done(((bf16[1024,1408]{1,0:T(8,128)(2,1)}), bf16[128,1408]{1,0:T(8,128)(2,1)}) %reduce-scatter.32.cloned.1.call-update) | async-done | bytes 360464
  394.5 63.0 %reduce-scatter.30.cloned.1.call-done = bf16[128,512]{1,0:T(8,128)(2,1)} async-done(((bf16[1024,512]{1,0:T(8,128)(2,1)}), bf16[128,512]{1,0:T(8,128)(2,1)}) %reduce-scatter.30.cloned.1.call-update) | async-done | bytes 131088
  460.1 23.7 %reduce-scatter.24.cloned.1.call-done = bf16[128,1024]{1,0:T(8,128)(2,1)} async-done(((bf16[512,1024]{1,0:T(8,128)(2,1)}), bf16[128,1024]{1,0:T(8,128)(2,1)}) %reduce-scatter.24.cloned.1.call-update) | async-done | bytes 262160 | tf_op jit(solution)/shard_map/reduce_scatter | solution.py:523
  485.5 38.4 %all-reduce.5 = (f32[1024]{0:T(1024)}, f32[4,2,512]{2,1,0:T(2,128)}, f32[2]{0:T(128)}, f32[2,256]{1,0:T(2,128)}, f32[1024]{0:T(1024)}) all-reduce(f32[1024]{0:T(1024)S(1)} %get-tuple-element.30, f32[4,2,512]{2,1,0:T(2,128)} %reshape.277, f32[2]{0:T(128)} %slice_reduce_fusion.1, ...), channel_id=6, replica_groups=mesh['dp'=8,'tensor'=4] {'dp'}, use_global_device_ids=true, to_apply=%region_12.13.clone | all-reduce | flops 6658 | bytes 53264
  526.1 6.4 %all-reduce.6 = (f32[128]{0:T(128)}, f32[128]{0:T(128)}) all-reduce(f32[128]{0:T(128)S(1)} %dynamic-slice.1, f32[128]{0:T(128)S(1)} %dynamic-slice.3), channel_id=1, replica_groups=mesh['dp'=8,'tensor'=4] {'tensor'}, use_global_device_ids=true, to_apply=%region_13.14 | all-reduce | flops 256 | bytes 2048 | tf_op jit(solution)/shard_map/psum | solution.py:549
  535.6 53.3 %reduce-scatter.26.cloned.1.call-done = bf16[128,1536]{1,0:T(8,128)(2,1)} async-done(((bf16[1024,1536]{1,0:T(8,128)(2,1)}), bf16[128,1536]{1,0:T(8,128)(2,1)}) %reduce-scatter.26.cloned.1.call-update) | async-done | bytes 393232 | tf_op jit(solution)/shard_map/reduce_scatter | solution.py:537
  (122 shorter events, 74.2 us)
Async XLA Ops:
  7.2 103.6 %copy-start = (bf16[1024,2,704]{0,2,1:T(8,128)(2,1)S(1)}, bf16[1024,2,704]{0,2,1:T(8,128)(2,1)}, u32[]{:S(2)}) copy-start(bf16[1024,2,704]{0,2,1:T(8,128)(2,1)} %param.23) | copy-start | bytes 8650756
  7.2 22.8 %all-gather.5.cloned.1.call-start = ((), (), s32[]{:S(2)}) async-start(), calls=%async_computation.9 | async-start | bytes 1310720 | tf_op jit(solution)/shard_map/all_gather | solution.py:467
  10.3 80.7 %reduce-scatter.18.cloned.1.call-start = ((), (), s32[]{:S(2)}) async-start(), calls=%async_computation.10 | async-start | bytes 1310720 | tf_op jit(solution)/shard_map/reduce_scatter | solution.py:476
  62.9 28.1 %copy-start.1 = (bf16[128,1024]{1,0:T(8,128)(2,1)S(1)}, bf16[128,1024]{1,0:T(8,128)(2,1)}, u32[]{:S(2)}) copy-start(bf16[128,1024]{1,0:T(8,128)(2,1)} %param.13) | copy-start | bytes 786436
  62.9 29.3 %copy-start.5 = (f32[1024]{0:T(1024)S(1)}, f32[1024]{0:T(1024)}, u32[]{:S(2)}) copy-start(f32[1024]{0:T(1024)} %param.22) | copy-start | bytes 12292
  66.1 44.7 %all-gather.7.cloned.1.call-start = ((), (), s32[]{:S(2)}) async-start(), calls=%async_computation.11 | async-start | bytes 1310720 | tf_op jit(solution)/shard_map/all_gather | solution.py:483
  92.1 70.9 %copy-start.8 = (f32[128]{0:T(128)}, f32[128]{0:T(128)S(1)}, u32[]{:S(2)}) copy-start(f32[128]{0:T(128)S(1)} %fusion.27) | copy-start | bytes 1540
  93.9 35.0 %all-gather.9.cloned.1.call-start = ((), (), s32[]{:S(2)}) async-start(), calls=%async_computation.13 | async-start | bytes 1310720 | tf_op jit(solution)/shard_map/all_gather | solution.py:495
  94.5 67.3 %reduce-scatter.22.cloned.1.call-start = ((), (), s32[]{:S(2)}) async-start(), calls=%async_computation.14 | async-start | bytes 1310720 | tf_op jit(solution)/shard_map/reduce_scatter | solution.py:502
  134.0 27.8 %copy-start.2 = (bf16[128,1024]{1,0:T(8,128)(2,1)S(1)}, bf16[128,1024]{1,0:T(8,128)(2,1)}, u32[]{:S(2)}) copy-start(bf16[128,1024]{1,0:T(8,128)(2,1)} %reduce-scatter.18.cloned.1.call-done) | copy-start | bytes 786436
  136.9 45.0 %all-gather.11.cloned.1.call-start = ((), (), s32[]{:S(2)}) async-start(), calls=%async_computation.15 | async-start | bytes 1310720 | tf_op jit(solution)/shard_map/all_gather | solution.py:511
  163.0 4.5 copy-start.10
  165.0 85.9 %reduce-scatter.34.cloned.1.call-start = ((), (), s32[]{:S(2)}) async-start(), calls=%async_computation.21 | async-start | bytes 1769472
  165.3 3.2 copy-start.12
  173.1 142.7 %reduce-scatter.28.cloned.1.call-start = ((), (), s32[]{:S(2)}) async-start(), calls=%async_computation.18 | async-start | bytes 589824
  214.6 176.1 %reduce-scatter.32.cloned.1.call-start = ((), (), s32[]{:S(2)}) async-start(), calls=%async_computation.20 | async-start | bytes 3244032
  224.2 233.2 %reduce-scatter.30.cloned.1.call-start = ((), (), s32[]{:S(2)}) async-start(), calls=%async_computation.19 | async-start | bytes 1179648
  233.5 250.2 %reduce-scatter.24.cloned.1.call-start = ((), (), s32[]{:S(2)}) async-start(), calls=%async_computation.16 | async-start | bytes 1310720 | tf_op jit(solution)/shard_map/reduce_scatter | solution.py:523
  233.6 4.2 copy-start.4
  239.2 294.0 %reduce-scatter.20.cloned.1.call-start = ((), (), s32[]{:S(2)}) async-start(), calls=%async_computation.12 | async-start | bytes 1310720 | tf_op jit(solution)/shard_map/reduce_scatter | solution.py:488
  242.9 346.0 %reduce-scatter.26.cloned.1.call-start = ((), (), s32[]{:S(2)}) async-start(), calls=%async_computation.17 | async-start | bytes 3538944 | tf_op jit(solution)/shard_map/reduce_scatter | solution.py:537
  248.4 5.9 copy-start.7
  248.4 6.6 %copy-start.13 = (f32[2,128]{1,0:T(2,128)S(1)}, f32[2,128]{1,0:T(2,128)}, u32[]{:S(2)}) copy-start(f32[2,128]{1,0:T(2,128)} %get-tuple-element.26) | copy-start | bytes 3076
  252.7 231.1 %copy-start.6 = (f32[1024]{0:T(1024)S(1)}, f32[1024]{0:T(1024)}, u32[]{:S(2)}) copy-start(f32[1024]{0:T(1024)} %param.15) | copy-start | bytes 12292
  (6 other events, 8.0 us)
Sparse Core Ops, SparseCore 0:
  10.4 19.4 all-gather.4
  66.2 24.7 reduce-scatter.17
  94.1 16.6 all-gather.6
  112.2 16.6 all-gather.8
  137.0 24.7 reduce-scatter.21
  165.1 16.6 all-gather.10
  185.3 65.6 reduce-scatter.33
  254.3 61.4 reduce-scatter.27
  319.3 71.3 reduce-scatter.31
  393.9 63.4 reduce-scatter.29
  460.0 23.7 reduce-scatter.23
  486.2 24.7 reduce-scatter.19
  514.6 74.3 reduce-scatter.25

commit v2 on v1

--- a/solution.py
+++ b/solution.py
@@ -473,6 +473,8 @@
     aux = jax.vmap(segment_ids, in_axes=(0, None))(seg_starts, length).reshape(total_rows, 8)
     mixer_args = (proj, gates_pre, aux, conv_w.reshape(4, -1), decay_rate[None, :], onorm_gain)
     mixed, states, inverses = mixer_forward(*mixer_args, dims, seqs)
+    cot_rows = lax.all_gather(cotangent, "tensor", axis=0, tiled=True)
+    mixed, cot_rows = lax.optimization_barrier((mixed, cot_rows))
     resid2 = resid + lax.psum_scatter(
         jnp.dot(mixed, out2d, preferred_element_type=f32).astype(jnp.bfloat16),
         "tensor",
@@ -483,22 +485,13 @@
     rows2 = lax.all_gather(normed2, "tensor", axis=0, tiled=True)
     gu = jnp.dot(rows2, gu2d, preferred_element_type=f32).reshape(total_rows, 2, hidden)
     act = swish_gate(gu[:, 0], gu[:, 1]).astype(bf16)
-    output = (
-        resid2
-        + lax.psum_scatter(
-            jnp.dot(act, w_down, preferred_element_type=f32).astype(jnp.bfloat16),
-            "tensor",
-            scatter_dimension=0,
-            tiled=True,
-        ).astype(jnp.float32)
-    ).astype(bf16)
-    cot_rows = lax.all_gather(cotangent, "tensor", axis=0, tiled=True)
-    grad_down = jnp.dot(act.T, cot_rows, preferred_element_type=f32)
+    ffn_part = jnp.dot(act, w_down, preferred_element_type=f32).astype(bf16)
+    grad_down = jnp.dot(cot_rows.T, act, preferred_element_type=f32).astype(bf16)
     d_act = jnp.dot(cot_rows, w_down.T, preferred_element_type=f32)
     _, swish_back = jax.vjp(swish_gate, gu[:, 0], gu[:, 1])
     d_gate, d_up = swish_back(d_act)
     d_gu = jnp.stack([d_gate, d_up], axis=1).astype(bf16).reshape(total_rows, 2 * hidden)
-    grad_gu = jnp.dot(rows2.T, d_gu, preferred_element_type=f32).reshape(width, 2, hidden)
+    grad_gu = jnp.dot(rows2.T, d_gu, preferred_element_type=f32).astype(bf16)
     d_normed2 = lax.psum_scatter(
         jnp.dot(d_gu, gu2d.T, preferred_element_type=f32).astype(jnp.bfloat16),
         "tensor",
@@ -509,17 +502,19 @@
     d_resid_ffn, gain2_part = norm2_back(d_normed2)
     d_resid2 = cotangent.astype(f32) + d_resid_ffn
     d_rows = lax.all_gather(d_resid2.astype(bf16), "tensor", axis=0, tiled=True)
-    grad_out = jnp.dot(mixed.T, d_rows, preferred_element_type=f32).reshape(
-        heads, value_width, width
-    )
+    grad_out = jnp.dot(d_rows.T, mixed, preferred_element_type=f32).astype(bf16)
     d_heads = jnp.dot(d_rows, out2d.T, preferred_element_type=f32)
+    d_heads, ffn_part = lax.optimization_barrier((d_heads, ffn_part))
+    ffn_sum = lax.psum_scatter(ffn_part, "tensor", scatter_dimension=0, tiled=True)
     d_proj_b, d_gates_b, d_conv, d_rate, d_onorm = mixer_backward(
         *mixer_args, states, inverses, d_heads, dims, seqs
     )
+    d_proj_b, ffn_sum = lax.optimization_barrier((d_proj_b, ffn_sum))
+    output = (resid2 + ffn_sum.astype(f32)).astype(bf16)
     d_conv = d_conv.reshape(conv_w.shape)
     d_rate = d_rate[:, 0]
-    grad_mix = jnp.dot(rows1.T, d_proj_b, preferred_element_type=f32)
-    grad_gates = jnp.dot(rows1.T, d_gates_b, preferred_element_type=f32).reshape(width, heads, 2)
+    grad_mix = jnp.dot(rows1.T, d_proj_b, preferred_element_type=f32).astype(bf16)
+    grad_gates = jnp.dot(rows1.T, d_gates_b, preferred_element_type=f32).astype(bf16)
     d_normed1 = lax.psum_scatter(
         (
             jnp.dot(d_proj_b, mix2d.T, preferred_element_type=f32)
@@ -529,23 +524,28 @@
         scatter_dimension=0,
         tiled=True,
     ).astype(jnp.float32)
+    d_normed1, grad_mix = lax.optimization_barrier((d_normed1, grad_mix))
     _, norm1_back = jax.vjp(rms_norm, resid, norm1_gain)
     d_resid1, gain1_part = norm1_back(d_normed1)
     grad_tokens = (d_resid2 + d_resid1).astype(bf16)
     grad_conv, grad_rate, grad_onorm = lax.psum((d_conv, d_rate, d_onorm), "dp")
-    mix_share, gates_share, out_share, gu_share, down_share, gain1_share, gain2_share = (
-        lax.psum_scatter(grad_mix.astype(bf16), "dp", scatter_dimension=0, tiled=True),
-        lax.psum_scatter(grad_gates, "dp", scatter_dimension=0, tiled=True),
-        lax.psum_scatter(grad_out.astype(bf16), "dp", scatter_dimension=2, tiled=True),
-        lax.psum_scatter(grad_gu.astype(bf16), "dp", scatter_dimension=0, tiled=True),
-        lax.psum_scatter(grad_down.astype(bf16), "dp", scatter_dimension=1, tiled=True),
-        lax.psum_scatter(gain1_part, "dp", scatter_dimension=0, tiled=True),
-        lax.psum_scatter(gain2_part, "dp", scatter_dimension=0, tiled=True),
+    pad = -(2 * heads) % 128
+    grads = jnp.concatenate(
+        [grad_mix, grad_gu, grad_down, grad_out, jnp.pad(grad_gates, ((0, 0), (0, pad)))], axis=1
     )
-    mix_share = mix_share.reshape(-1, heads, mix_cols)
-    mix_share, out_share, gu_share, down_share = (
-        share.astype(f32) for share in (mix_share, out_share, gu_share, down_share)
-    )
+    shares = lax.psum_scatter(grads, "dp", scatter_dimension=0, tiled=True).astype(f32)
+    cuts = []
+    place = 0
+    for size in (heads * mix_cols, 2 * hidden, hidden, heads * value_width, 2 * heads):
+        cuts.append(shares[:, place : place + size])
+        place += size
+    mix_share = cuts[0].reshape(-1, heads, mix_cols)
+    gu_share = cuts[1].reshape(-1, 2, hidden)
+    down_share = cuts[2].T
+    out_share = cuts[3].T.reshape(heads, value_width, -1)
+    gates_share = cuts[4].reshape(-1, heads, 2)
+    gain1_share = lax.psum_scatter(gain1_part, "dp", scatter_dimension=0, tiled=True)
+    gain2_share = lax.psum_scatter(gain2_part, "dp", scatter_dimension=0, tiled=True)
     gain1_total, gain2_total = lax.psum((gain1_share, gain2_share), "tensor")
     return (
         output,

time: 599 us -> 413 us (0.69)
  waiting for transfers between devices: 373 us -> 202 us
  matrix products: 52.9 us -> 42.7 us
    unnamed x17 -> x9, waiting for transfers between devices: 198 us -> 0.83 us
    reduce_scatter x2, waiting for transfers between devices: 53.3 us -> 106 us  [the longest x1 106 us: local(): lax.psum_scatter(grads, 'dp', scatter_dimension=0, tiled=True).astype(f32)]
    unnamed x48 -> x86, local copies, waits for them, and re-layouts: 31.2 us -> 11.5 us
    reduce_scatter x1, waiting for transfers between devices: 23.7 us -> 7.28 us  [local(): lax.psum_scatter((jnp.dot(d_proj_b, mix2d.T, preferred_element_type=f32)...]
    concatenate x0 -> x1, local copies, waits for them, and re-layouts: none -> 13.7 us  [local(): jnp.concatenate([grad_mix, grad_gu, grad_down, grad_out, jnp.pad(grad_gat...]
    all_gather x1, waiting for transfers between devices: 13.6 us -> 0.02 us  [local(): cot_rows = lax.all_gather(cotangent, 'tensor', axis=0, tiled=True)]
    dot_general x5 -> x6, matrix products: 19 us -> 15.6 us  [the longest x1 3.51 us: local(): jnp.dot(rows1.T, d_proj_b, preferred_element_type=f32).astype(bf16)]
  transfers between devices with their start and end apart: 13 -> 9, of which waited for: 12 -> 7; matrix products, arithmetic and copies ran while one was open for 14% -> 10% of each run, Pallas kernels for 4% -> 13%
where the time goes in v2:
time: 413 us; the launch traced here: 412 us
  waiting for transfers between devices  202 us (49%)
  Pallas kernels  51.9 us (13%)
  blocking collectives  46.4 us (11%)
  matrix products  42.7 us (10%)
  local copies, waits for them, and re-layouts  36.5 us (9%)
  other arithmetic  16.8 us (4%)
  between operations  15 us (4%)
    reduce_scatter x1, waiting for transfers between devices, local(): lax.psum_scatter(grads, 'dp', scatter_dimension=0, tiled=True).astype(f32)  106 us
    unnamed x1, blocking collectives  39.9 us
    pallas_call x1, Pallas kernels, mixer_backward(): pl.pallas_call(functools.partial(backward_kernel, dims), grid=(seqs, bloc...  26.9 us
    pallas_call x1, Pallas kernels, mixer_forward(): pl.pallas_call(functools.partial(forward_kernel, dims), grid=(seqs, block...  24.9 us
    reduce_scatter x1, waiting for transfers between devices, local(): lax.psum_scatter(jnp.dot(d_gu, gu2d.T, preferred_element_type=f32).astype...  24.9 us
    reduce_scatter x1, waiting for transfers between devices, local(): lax.psum_scatter(jnp.dot(mixed, out2d, preferred_element_type=f32).astype...  24.9 us
    all_gather x1, waiting for transfers between devices, local(): rows2 = lax.all_gather(normed2, 'tensor', axis=0, tiled=True)  16.8 us
    concatenate x1, local copies, waits for them, and re-layouts, local(): jnp.concatenate([grad_mix, grad_gu, grad_down, grad_out, jnp.pad(grad_gat...  13.7 us
  transfers between devices with their start and end apart: 9, of which 7 were waited for; matrix products, arithmetic and copies ran while one was open for 10% of the time, Pallas kernels for 13%

profile of v2, /device:TPU:0, one launch (start us, length us, event | category | flops | bytes accessed | tf_op | source)
XLA Modules:
  0.0 412.0 jit_solution(5349948408878482099)
XLA Ops:
  17.2 4.2 %copy.83 = bf16[128,8,2,768]{3,1,2,0:T(8,128)(2,1)} copy(bf16[128,8,2,768]{3,2,1,0:T(2,128)(2,1)} %bitcast.95) | data formatting | bytes 6291456
  21.3 8.5 %all-gather.5.cloned.1.call-done = bf16[512,1024]{1,0:T(8,128)(2,1)} async-done(((bf16[128,1024]{1,0:T(8,128)(2,1)}), bf16[512,1024]{1,0:T(8,128)(2,1)}) %all-gather.5.cloned.1.call-update) | async-done | bytes 1048592 | tf_op jit(solution)/shard_map/all_gather | solution.py:467
  32.2 5.7 %fusion.27.halo_ref.proj_ref = f32[512,1536]{1,0:T(8,128)} fusion(bf16[512,1024]{1,0:T(8,128)(2,1)} %all-gather.5.cloned.1.call-done, bf16[1024,1536]{1,0:T(8,128)(2,1)} %bitcast.96), kind=kOutput, calls=%fused_computation.75 | convolution fusion | flops 1610612736 | bytes 7340032 | tf_op jit(solution)/shard_map/dot_general | solution.py:471
  37.9 24.9 %mixer_forward.1 = (bf16[512,512]{1,0:T(8,128)(2,1)}, f32[8,256,256]{2,1,0:T(8,128)}, f32[8,128,64]{2,1,0:T(8,128)}) custom-call(f32[512,1536]{1,0:T(8,128)} %fusion.27.halo_ref.proj_ref, f32[512,1536]{1,0:T(8,128)} %fusion.27.halo_ref.proj_ref, f32[512,4]{1,0:T(8,128)} %fusion.28.gates_ref, f32[512,8]{1,0:T(8,128)} %bitcast.100, f32[4,1024]{1,0:T(4,128)} %bitcast.111, ...), custom_call_target="tpu_custom_call" | custom-call | flops 2048000000 | bytes 8388608 | tf_op jit(solution)/shard_map/mixer_forward/pallas_call | solution.py:375
  62.9 3.1 convolution_convert_fusion.5
  66.1 24.9 %reduce-scatter.6.cloned.1.call-done = bf16[128,1024]{1,0:T(8,128)(2,1)} async-done(((bf16[512,1024]{1,0:T(8,128)(2,1)}), bf16[128,1024]{1,0:T(8,128)(2,1)}) %reduce-scatter.6.cloned.1.call-update) | async-done | bytes 262160 | tf_op jit(solution)/shard_map/reduce_scatter | solution.py:478
  94.0 16.8 %all-gather.9.cloned.1.call-done = bf16[512,1024]{1,0:T(8,128)(2,1)} async-done(((bf16[128,1024]{1,0:T(8,128)(2,1)}), bf16[512,1024]{1,0:T(8,128)(2,1)}) %all-gather.9.cloned.1.call-update) | async-done | bytes 1048592 | tf_op jit(solution)/shard_map/all_gather | solution.py:485
  110.8 3.1 fusion
  116.5 2.9 bitcast_convert_fusion
  119.5 24.9 %reduce-scatter.8.cloned.1.call-done = bf16[128,1024]{1,0:T(8,128)(2,1)} async-done(((bf16[512,1024]{1,0:T(8,128)(2,1)}), bf16[128,1024]{1,0:T(8,128)(2,1)}) %reduce-scatter.8.cloned.1.call-update) | async-done | bytes 262160 | tf_op jit(solution)/shard_map/reduce_scatter | solution.py:495
  151.2 13.3 %all-gather.11.cloned.1.call-done = bf16[512,1024]{1,0:T(8,128)(2,1)} async-done(((bf16[128,1024]{1,0:T(8,128)(2,1)}), bf16[512,1024]{1,0:T(8,128)(2,1)}) %all-gather.11.cloned.1.call-update) | async-done | bytes 1048592 | tf_op jit(solution)/shard_map/all_gather | solution.py:504
  164.5 3.0 fusion.29.d_out_ref
  167.5 26.9 %mixer_backward.1 = (bf16[512,1536]{1,0:T(8,128)(2,1)}, bf16[512,4]{1,0:T(8,128)(2,1)}, f32[4,1024]{1,0:T(4,128)}, f32[2,128]{1,0:T(2,128)}, f32[2,256]{1,0:T(2,128)}) custom-call(f32[512,1536]{1,0:T(8,128)} %fusion.27.halo_ref.proj_ref, f32[512,1536]{1,0:T(8,128)} %fusion.27.halo_ref.proj_ref, f32[512,4]{1,0:T(8,128)} %fusion.28.gates_ref, ...), custom_call_target="tpu_custom_call" | custom-call | flops 5120000000 | bytes 12582912 | tf_op jit(solution)/shard_map/mixer_backward/pallas_call | solution.py:402
  194.5 4.2 %fusion.30 = f32[512,1024]{1,0:T(8,128)S(1)} fusion(bf16[512,1536]{1,0:T(8,128)(2,1)} %get-tuple-element.37, bf16[1024,1536]{1,0:T(8,128)(2,1)} %bitcast.97), kind=kOutput, calls=%fused_computation.78 | convolution fusion | flops 1610612736 | bytes 6815744 | tf_op jit(solution)/shard_map/dot_general | solution.py:520
  200.2 3.3 convolution_convert_fusion.2
  206.7 3.4 convolution_convert_fusion
  211.2 3.1 convolution_convert_fusion.4
  214.3 3.5 convolution_convert_fusion.1
  217.8 7.3 %reduce-scatter.12.cloned.1.call-done = bf16[128,1024]{1,0:T(8,128)(2,1)} async-done(((bf16[512,1024]{1,0:T(8,128)(2,1)}), bf16[128,1024]{1,0:T(8,128)(2,1)}) %reduce-scatter.12.cloned.1.call-update) | async-done | bytes 262160 | tf_op jit(solution)/shard_map/reduce_scatter | solution.py:518
  226.1 13.7 %concatenate.7 = bf16[1024,4288]{1,0:T(8,128)(2,1)} concatenate(bf16[1024,1536]{1,0:T(8,128)(2,1)} %convolution_convert_fusion.1, bf16[1024,1408]{1,0:T(8,128)(2,1)} %convolution_convert_fusion, bf16[1024,704]{1,0:T(8,128)(2,1)S(1)} %copy.73, bf16[1024,512]{1,0:T(8,128)(2,1)} %convolution_convert_fusion.4, bf16[1024,128]{1,0:T(8,128)(2,1)S(1)} %pad.19.clone), dimensions={1} | concatenate | bytes 17563648 | tf_op jit(solution)/shard_map/concatenate | solution.py:533
  242.1 39.9 %all-reduce.6 = (f32[1024]{0:T(1024)S(1)}, f32[4,2,512]{2,1,0:T(2,128)}, f32[2]{0:T(128)}, f32[2,256]{1,0:T(2,128)}, f32[1024]{0:T(1024)S(1)}) all-reduce(f32[1024]{0:T(1024)S(1)} %get-tuple-element.106, f32[4,2,512]{2,1,0:T(2,128)S(1)} %reshape.280, f32[2]{0:T(128)S(1)} %slice_reduce_fusion.1, ...), channel_id=6, replica_groups=mesh['dp'=8,'tensor'=4] {'dp'}, use_global_device_ids=true, to_apply=%region_12.13.clone | all-reduce | flops 6658 | bytes 53264
  282.1 6.5 %all-reduce.7 = (f32[128]{0:T(128)}, f32[128]{0:T(128)}) all-reduce(f32[128]{0:T(128)S(1)} %dynamic-slice.1, f32[128]{0:T(128)S(1)} %dynamic-slice.3), channel_id=1, replica_groups=mesh['dp'=8,'tensor'=4] {'tensor'}, use_global_device_ids=true, to_apply=%region_13.14 | all-reduce | flops 256 | bytes 2048 | tf_op jit(solution)/shard_map/psum | solution.py:549
  289.9 105.7 %reduce-scatter.14.cloned.1.call-done = bf16[128,4288]{1,0:T(8,128)(2,1)} async-done(((bf16[1024,4288]{1,0:T(8,128)(2,1)}), bf16[128,4288]{1,0:T(8,128)(2,1)}) %reduce-scatter.14.cloned.1.call-update) | async-done | bytes 1097744 | tf_op jit(solution)/shard_map/reduce_scatter | solution.py:536
  401.2 2.5 reshape.278
  (158 shorter events, 41.7 us)
Async XLA Ops:
  7.2 103.6 %copy-start = (bf16[1024,2,704]{0,2,1:T(8,128)(2,1)S(1)}, bf16[1024,2,704]{0,2,1:T(8,128)(2,1)}, u32[]{:S(2)}) copy-start(bf16[1024,2,704]{0,2,1:T(8,128)(2,1)} %param.23) | copy-start | bytes 8650756
  7.2 22.7 %all-gather.5.cloned.1.call-start = ((), (), s32[]{:S(2)}) async-start(), calls=%async_computation.5 | async-start | bytes 1310720 | tf_op jit(solution)/shard_map/all_gather | solution.py:467
  10.3 52.6 %all-gather.7.cloned.1.call-start = ((), (), s32[]{:S(2)}) async-start(), calls=%async_computation.6 | async-start | bytes 1310720 | tf_op jit(solution)/shard_map/all_gather | solution.py:476
  11.1 79.9 %reduce-scatter.6.cloned.1.call-start = ((), (), s32[]{:S(2)}) async-start(), calls=%async_computation.7 | async-start | bytes 1310720 | tf_op jit(solution)/shard_map/reduce_scatter | solution.py:478
  62.9 28.1 %copy-start.2 = (bf16[128,1024]{1,0:T(8,128)(2,1)S(1)}, bf16[128,1024]{1,0:T(8,128)(2,1)}, u32[]{:S(2)}) copy-start(bf16[128,1024]{1,0:T(8,128)(2,1)} %param.13) | copy-start | bytes 786436
  62.9 29.2 %copy-start.18 = (f32[1024]{0:T(1024)S(1)}, f32[1024]{0:T(1024)}, u32[]{:S(2)}) copy-start(f32[1024]{0:T(1024)} %param.22) | copy-start | bytes 12292
  66.0 44.7 %all-gather.9.cloned.1.call-start = ((), (), s32[]{:S(2)}) async-start(), calls=%async_computation.8 | async-start | bytes 1310720 | tf_op jit(solution)/shard_map/all_gather | solution.py:485
  92.1 53.5 %copy-start.21 = (f32[128]{0:T(128)}, f32[128]{0:T(128)S(1)}, u32[]{:S(2)}) copy-start(f32[128]{0:T(128)S(1)} %fusion.25) | copy-start | bytes 1540
  93.9 50.5 %reduce-scatter.8.cloned.1.call-start = ((), (), s32[]{:S(2)}) async-start(), calls=%async_computation.9 | async-start | bytes 1310720 | tf_op jit(solution)/shard_map/reduce_scatter | solution.py:495
  116.5 27.9 %copy-start.3 = (bf16[128,1024]{1,0:T(8,128)(2,1)S(1)}, bf16[128,1024]{1,0:T(8,128)(2,1)}, u32[]{:S(2)}) copy-start(bf16[128,1024]{1,0:T(8,128)(2,1)} %reduce-scatter.6.cloned.1.call-done) | copy-start | bytes 786436
  119.4 28.4 %copy-start.8 = (f32[512,2,704]{0,2,1:T(8,128)S(1)}, f32[512,2,704]{0,2,1:T(8,128)}, u32[]{:S(2)}) copy-start(f32[512,2,704]{0,2,1:T(8,128)} %copy-done.7) | copy-start | bytes 8650756
  119.5 45.0 %all-gather.11.cloned.1.call-start = ((), (), s32[]{:S(2)}) async-start(), calls=%async_computation.10 | async-start | bytes 1310720 | tf_op jit(solution)/shard_map/all_gather | solution.py:504
  147.6 46.9 %reduce-scatter.10.cloned.1.call-start = ((), (), s32[]{:S(2)}) async-start(), calls=%async_computation.11 | async-start | bytes 1310720 | tf_op jit(solution)/shard_map/reduce_scatter | solution.py:508
  149.2 15.2 %copy-start.32 = (bf16[2,256,1024]{2,1,0:T(8,128)(2,1)S(1)}, bf16[2,256,1024]{2,1,0:T(8,128)(2,1)}, u32[]{:S(2)}) copy-start(bf16[2,256,1024]{2,1,0:T(8,128)(2,1)} %param.21) | copy-start | bytes 3145732
  167.5 57.6 %reduce-scatter.12.cloned.1.call-start = ((), (), s32[]{:S(2)}) async-start(), calls=%async_computation.12 | async-start | bytes 1310720 | tf_op jit(solution)/shard_map/reduce_scatter | solution.py:518
  194.5 4.2 %copy-start.16 = (bf16[512,4]{1,0:T(8,128)(2,1)S(1)}, bf16[512,4]{1,0:T(8,128)(2,1)}, u32[]{:S(2)}) copy-start(bf16[512,4]{1,0:T(8,128)(2,1)} %get-tuple-element.38) | copy-start | bytes 12292
  200.1 195.4 %reduce-scatter.14.cloned.1.call-start = ((), (), s32[]{:S(2)}) async-start(), calls=%async_computation.13 | async-start | bytes 10027008 | tf_op jit(solution)/shard_map/reduce_scatter | solution.py:536
  239.8 48.8 %copy-start.29 = (f32[128]{0:T(128)S(1)}, f32[128]{0:T(128)}, u32[]{:S(2)}) copy-start(f32[128]{0:T(128)} %copy-done.28) | copy-start | bytes 1540
  239.8 48.8 %copy-start.9 = (bf16[128,1024]{1,0:T(8,128)(2,1)S(1)}, bf16[128,1024]{1,0:T(8,128)(2,1)}, u32[]{:S(2)}) copy-start(bf16[128,1024]{1,0:T(8,128)(2,1)} %param.25) | copy-start | bytes 786436
  239.9 48.8 %copy-start.10 = (bf16[128,1024]{1,0:T(8,128)(2,1)S(1)}, bf16[128,1024]{1,0:T(8,128)(2,1)}, u32[]{:S(2)}) copy-start(bf16[128,1024]{1,0:T(8,128)(2,1)} %reduce-scatter.8.cloned.1.call-done) | copy-start | bytes 786436
  239.9 48.8 %copy-start.17 = (bf16[128,1024]{1,0:T(8,128)(2,1)S(1)}, bf16[128,1024]{1,0:T(8,128)(2,1)}, u32[]{:S(2)}) copy-start(bf16[128,1024]{1,0:T(8,128)(2,1)} %reduce-scatter.10.cloned.1.call-done) | copy-start | bytes 786436
  239.9 48.8 %copy-start.22 = (f32[128]{0:T(128)S(1)}, f32[128]{0:T(128)}, u32[]{:S(2)}) copy-start(f32[128]{0:T(128)} %copy-done.21) | copy-start | bytes 1540
  239.9 48.8 %copy-start.27 = (f32[128]{0:T(128)S(1)}, f32[128]{0:T(128)}, u32[]{:S(2)}) copy-start(f32[128]{0:T(128)} %copy-done.26) | copy-start | bytes 1540
  399.1 6.4 %copy-start.1 = (bf16[1024,2,704]{0,2,1:T(8,128)(2,1)S(1)}, bf16[1024,2,704]{0,2,1:T(8,128)(2,1)}, u32[]{:S(2)}) copy-start(bf16[1024,2,704]{0,2,1:T(8,128)(2,1)} %param.23) | copy-start | bytes 8650756
  (24 other events, 48.5 us)
Sparse Core Ops, SparseCore 0:
  10.4 19.4 all-gather.4
  31.5 16.6 all-gather.6
  66.2 24.7 reduce-scatter.5
  94.0 16.6 all-gather.8
  119.6 24.7 reduce-scatter.7
  147.7 16.6 all-gather.10
  167.6 24.7 reduce-scatter.9
  200.2 24.7 reduce-scatter.11
  240.0 155.4 reduce-scatter.13

commit v3 on v2

--- a/solution.py
+++ b/solution.py
@@ -524,15 +524,15 @@
         scatter_dimension=0,
         tiled=True,
     ).astype(jnp.float32)
-    d_normed1, grad_mix = lax.optimization_barrier((d_normed1, grad_mix))
+    pad = -(2 * heads) % 128
+    grads = jnp.concatenate(
+        [grad_mix, grad_gu, grad_down, grad_out, jnp.pad(grad_gates, ((0, 0), (0, pad)))], axis=1
+    )
+    d_normed1, grads = lax.optimization_barrier((d_normed1, grads))
     _, norm1_back = jax.vjp(rms_norm, resid, norm1_gain)
     d_resid1, gain1_part = norm1_back(d_normed1)
     grad_tokens = (d_resid2 + d_resid1).astype(bf16)
     grad_conv, grad_rate, grad_onorm = lax.psum((d_conv, d_rate, d_onorm), "dp")
-    pad = -(2 * heads) % 128
-    grads = jnp.concatenate(
-        [grad_mix, grad_gu, grad_down, grad_out, jnp.pad(grad_gates, ((0, 0), (0, pad)))], axis=1
-    )
     shares = lax.psum_scatter(grads, "dp", scatter_dimension=0, tiled=True).astype(f32)
     cuts = []
     place = 0

time: 413 us -> 407 us (0.985)
  waiting for transfers between devices: 202 us -> 195 us
    reduce_scatter x1, waiting for transfers between devices: 7.28 us -> 0.01 us  [local(): lax.psum_scatter((jnp.dot(d_proj_b, mix2d.T, preferred_element_type=f32)...]
    unnamed x86 -> x82, local copies, waits for them, and re-layouts: 11.5 us -> 11.7 us
  transfers between devices with their start and end apart: 9 -> 9, of which waited for: 7 -> 6; matrix products, arithmetic and copies ran while one was open for 10% -> 14% of each run, Pallas kernels for 13% -> 13%
where the time goes in v3:
time: 407 us; the launch traced here: 406 us
  waiting for transfers between devices  195 us (48%)
  Pallas kernels  51.8 us (13%)
  blocking collectives  46.6 us (11%)
  matrix products  42.8 us (11%)
  local copies, waits for them, and re-layouts  37.7 us (9%)
  other arithmetic  16.8 us (4%)
  between operations  15 us (4%)
    reduce_scatter x1, waiting for transfers between devices, local(): lax.psum_scatter(grads, 'dp', scatter_dimension=0, tiled=True).astype(f32)  106 us
    unnamed x1, blocking collectives  40 us
    pallas_call x1, Pallas kernels, mixer_backward(): pl.pallas_call(functools.partial(backward_kernel, dims), grid=(seqs, bloc...  26.9 us
    reduce_scatter x1, waiting for transfers between devices, local(): lax.psum_scatter(jnp.dot(mixed, out2d, preferred_element_type=f32).astype...  24.9 us
    pallas_call x1, Pallas kernels, mixer_forward(): pl.pallas_call(functools.partial(forward_kernel, dims), grid=(seqs, block...  24.9 us
    reduce_scatter x1, waiting for transfers between devices, local(): lax.psum_scatter(jnp.dot(d_gu, gu2d.T, preferred_element_type=f32).astype...  24.9 us
    all_gather x1, waiting for transfers between devices, local(): rows2 = lax.all_gather(normed2, 'tensor', axis=0, tiled=True)  16.8 us
    concatenate x1, local copies, waits for them, and re-layouts, local(): jnp.concatenate([grad_mix, grad_gu, grad_down, grad_out, jnp.pad(grad_gat...  13.7 us
  transfers between devices with their start and end apart: 9, of which 6 were waited for; matrix products, arithmetic and copies ran while one was open for 14% of the time, Pallas kernels for 13%

profile of v3, /device:TPU:0, one launch (start us, length us, event | category | flops | bytes accessed | tf_op | source)
XLA Modules:
  0.0 406.0 jit_solution(492660269775440285)
XLA Ops:
  17.2 4.1 %copy.83 = bf16[128,8,2,768]{3,1,2,0:T(8,128)(2,1)} copy(bf16[128,8,2,768]{3,2,1,0:T(2,128)(2,1)} %bitcast.95) | data formatting | bytes 6291456
  21.3 8.6 %all-gather.5.cloned.1.call-done = bf16[512,1024]{1,0:T(8,128)(2,1)} async-done(((bf16[128,1024]{1,0:T(8,128)(2,1)}), bf16[512,1024]{1,0:T(8,128)(2,1)}) %all-gather.5.cloned.1.call-update) | async-done | bytes 1048592 | tf_op jit(solution)/shard_map/all_gather | solution.py:467
  29.9 2.3 fusion.28.gates_ref
  32.2 5.7 %fusion.27.halo_ref.proj_ref = f32[512,1536]{1,0:T(8,128)} fusion(bf16[512,1024]{1,0:T(8,128)(2,1)} %all-gather.5.cloned.1.call-done, bf16[1024,1536]{1,0:T(8,128)(2,1)} %bitcast.96), kind=kOutput, calls=%fused_computation.75 | convolution fusion | flops 1610612736 | bytes 7340032 | tf_op jit(solution)/shard_map/dot_general | solution.py:471
  37.9 24.9 %mixer_forward.1 = (bf16[512,512]{1,0:T(8,128)(2,1)}, f32[8,256,256]{2,1,0:T(8,128)}, f32[8,128,64]{2,1,0:T(8,128)}) custom-call(f32[512,1536]{1,0:T(8,128)} %fusion.27.halo_ref.proj_ref, f32[512,1536]{1,0:T(8,128)} %fusion.27.halo_ref.proj_ref, f32[512,4]{1,0:T(8,128)} %fusion.28.gates_ref, f32[512,8]{1,0:T(8,128)} %bitcast.100, f32[4,1024]{1,0:T(4,128)} %bitcast.111, ...), custom_call_target="tpu_custom_call" | custom-call | flops 2048000000 | bytes 8388608 | tf_op jit(solution)/shard_map/mixer_forward/pallas_call | solution.py:375
  62.9 3.2 convolution_convert_fusion.5
  66.1 24.9 %reduce-scatter.6.cloned.1.call-done = bf16[128,1024]{1,0:T(8,128)(2,1)} async-done(((bf16[512,1024]{1,0:T(8,128)(2,1)}), bf16[128,1024]{1,0:T(8,128)(2,1)}) %reduce-scatter.6.cloned.1.call-update) | async-done | bytes 262160 | tf_op jit(solution)/shard_map/reduce_scatter | solution.py:478
  94.0 16.8 %all-gather.9.cloned.1.call-done = bf16[512,1024]{1,0:T(8,128)(2,1)} async-done(((bf16[128,1024]{1,0:T(8,128)(2,1)}), bf16[512,1024]{1,0:T(8,128)(2,1)}) %all-gather.9.cloned.1.call-update) | async-done | bytes 1048592 | tf_op jit(solution)/shard_map/all_gather | solution.py:485
  110.9 3.1 fusion
  116.7 2.8 bitcast_convert_fusion
  119.6 24.9 %reduce-scatter.8.cloned.1.call-done = bf16[128,1024]{1,0:T(8,128)(2,1)} async-done(((bf16[512,1024]{1,0:T(8,128)(2,1)}), bf16[128,1024]{1,0:T(8,128)(2,1)}) %reduce-scatter.8.cloned.1.call-update) | async-done | bytes 262160 | tf_op jit(solution)/shard_map/reduce_scatter | solution.py:495
  151.3 13.2 %all-gather.11.cloned.1.call-done = bf16[512,1024]{1,0:T(8,128)(2,1)} async-done(((bf16[128,1024]{1,0:T(8,128)(2,1)}), bf16[512,1024]{1,0:T(8,128)(2,1)}) %all-gather.11.cloned.1.call-update) | async-done | bytes 1048592 | tf_op jit(solution)/shard_map/all_gather | solution.py:504
  164.5 2.9 fusion.29.d_out_ref
  167.5 26.9 %mixer_backward.1 = (bf16[512,1536]{1,0:T(8,128)(2,1)}, bf16[512,4]{1,0:T(8,128)(2,1)}, f32[4,1024]{1,0:T(4,128)}, f32[2,128]{1,0:T(2,128)}, f32[2,256]{1,0:T(2,128)}) custom-call(f32[512,1536]{1,0:T(8,128)} %fusion.27.halo_ref.proj_ref, f32[512,1536]{1,0:T(8,128)} %fusion.27.halo_ref.proj_ref, f32[512,4]{1,0:T(8,128)} %fusion.28.gates_ref, ...), custom_call_target="tpu_custom_call" | custom-call | flops 5120000000 | bytes 12582912 | tf_op jit(solution)/shard_map/mixer_backward/pallas_call | solution.py:402
  194.5 4.2 %fusion.30 = f32[512,1024]{1,0:T(8,128)S(1)} fusion(bf16[512,1536]{1,0:T(8,128)(2,1)} %get-tuple-element.37, bf16[1024,1536]{1,0:T(8,128)(2,1)} %bitcast.97), kind=kOutput, calls=%fused_computation.78 | convolution fusion | flops 1610612736 | bytes 6815744 | tf_op jit(solution)/shard_map/dot_general | solution.py:520
  200.2 3.2 convolution_convert_fusion.2
  206.7 3.4 convolution_convert_fusion
  212.3 3.2 convolution_convert_fusion.4
  215.6 3.5 convolution_convert_fusion.1
  219.0 13.7 %concatenate.7 = bf16[1024,4288]{1,0:T(8,128)(2,1)} concatenate(bf16[1024,1536]{1,0:T(8,128)(2,1)} %convolution_convert_fusion.1, bf16[1024,1408]{1,0:T(8,128)(2,1)} %convolution_convert_fusion, bf16[1024,704]{1,0:T(8,128)(2,1)S(1)} %copy.73, bf16[1024,512]{1,0:T(8,128)(2,1)} %convolution_convert_fusion.4, bf16[1024,128]{1,0:T(8,128)(2,1)S(1)} %pad.19.clone), dimensions={1} | concatenate | bytes 17563648 | tf_op jit(solution)/shard_map/concatenate | solution.py:528
  236.1 40.0 %all-reduce.6 = (f32[1024]{0:T(1024)S(1)}, f32[4,2,512]{2,1,0:T(2,128)}, f32[2]{0:T(128)}, f32[2,256]{1,0:T(2,128)}, f32[1024]{0:T(1024)S(1)}) all-reduce(f32[1024]{0:T(1024)S(1)} %get-tuple-element.106, f32[4,2,512]{2,1,0:T(2,128)S(1)} %reshape.280, f32[2]{0:T(128)S(1)} %slice_reduce_fusion.1, ...), channel_id=6, replica_groups=mesh['dp'=8,'tensor'=4] {'dp'}, use_global_device_ids=true, to_apply=%region_12.13.clone | all-reduce | flops 6658 | bytes 53264
  276.2 6.5 %all-reduce.7 = (f32[128]{0:T(128)}, f32[128]{0:T(128)}) all-reduce(f32[128]{0:T(128)S(1)} %dynamic-slice.1, f32[128]{0:T(128)S(1)} %dynamic-slice.3), channel_id=1, replica_groups=mesh['dp'=8,'tensor'=4] {'tensor'}, use_global_device_ids=true, to_apply=%region_13.14 | all-reduce | flops 256 | bytes 2048 | tf_op jit(solution)/shard_map/psum | solution.py:549
  284.0 105.5 %reduce-scatter.14.cloned.1.call-done = bf16[128,4288]{1,0:T(8,128)(2,1)} async-done(((bf16[1024,4288]{1,0:T(8,128)(2,1)}), bf16[128,4288]{1,0:T(8,128)(2,1)}) %reduce-scatter.14.cloned.1.call-update) | async-done | bytes 1097744 | tf_op jit(solution)/shard_map/reduce_scatter | solution.py:536
  395.2 2.5 reshape.278
  (154 shorter events, 40.6 us)
Async XLA Ops:
  7.2 103.7 %copy-start = (bf16[1024,2,704]{0,2,1:T(8,128)(2,1)S(1)}, bf16[1024,2,704]{0,2,1:T(8,128)(2,1)}, u32[]{:S(2)}) copy-start(bf16[1024,2,704]{0,2,1:T(8,128)(2,1)} %param.23) | copy-start | bytes 8650756
  7.2 22.7 %all-gather.5.cloned.1.call-start = ((), (), s32[]{:S(2)}) async-start(), calls=%async_computation.5 | async-start | bytes 1310720 | tf_op jit(solution)/shard_map/all_gather | solution.py:467
  10.3 52.5 %all-gather.7.cloned.1.call-start = ((), (), s32[]{:S(2)}) async-start(), calls=%async_computation.6 | async-start | bytes 1310720 | tf_op jit(solution)/shard_map/all_gather | solution.py:476
  11.1 80.0 %reduce-scatter.6.cloned.1.call-start = ((), (), s32[]{:S(2)}) async-start(), calls=%async_computation.7 | async-start | bytes 1310720 | tf_op jit(solution)/shard_map/reduce_scatter | solution.py:478
  62.9 28.2 %copy-start.2 = (bf16[128,1024]{1,0:T(8,128)(2,1)S(1)}, bf16[128,1024]{1,0:T(8,128)(2,1)}, u32[]{:S(2)}) copy-start(bf16[128,1024]{1,0:T(8,128)(2,1)} %param.13) | copy-start | bytes 786436
  62.9 29.3 %copy-start.17 = (f32[1024]{0:T(1024)S(1)}, f32[1024]{0:T(1024)}, u32[]{:S(2)}) copy-start(f32[1024]{0:T(1024)} %param.22) | copy-start | bytes 12292
  66.1 44.8 %all-gather.9.cloned.1.call-start = ((), (), s32[]{:S(2)}) async-start(), calls=%async_computation.8 | async-start | bytes 1310720 | tf_op jit(solution)/shard_map/all_gather | solution.py:485
  92.2 53.5 %copy-start.20 = (f32[128]{0:T(128)}, f32[128]{0:T(128)S(1)}, u32[]{:S(2)}) copy-start(f32[128]{0:T(128)S(1)} %fusion.25) | copy-start | bytes 1540
  94.0 50.5 %reduce-scatter.8.cloned.1.call-start = ((), (), s32[]{:S(2)}) async-start(), calls=%async_computation.9 | async-start | bytes 1310720 | tf_op jit(solution)/shard_map/reduce_scatter | solution.py:495
  116.7 27.8 %copy-start.3 = (bf16[128,1024]{1,0:T(8,128)(2,1)S(1)}, bf16[128,1024]{1,0:T(8,128)(2,1)}, u32[]{:S(2)}) copy-start(bf16[128,1024]{1,0:T(8,128)(2,1)} %reduce-scatter.6.cloned.1.call-done) | copy-start | bytes 786436
  119.5 28.4 %copy-start.7 = (f32[512,2,704]{0,2,1:T(8,128)S(1)}, f32[512,2,704]{0,2,1:T(8,128)}, u32[]{:S(2)}) copy-start(f32[512,2,704]{0,2,1:T(8,128)} %copy-done.6) | copy-start | bytes 8650756
  119.5 45.0 %all-gather.11.cloned.1.call-start = ((), (), s32[]{:S(2)}) async-start(), calls=%async_computation.10 | async-start | bytes 1310720 | tf_op jit(solution)/shard_map/all_gather | solution.py:504
  147.7 46.8 %reduce-scatter.10.cloned.1.call-start = ((), (), s32[]{:S(2)}) async-start(), calls=%async_computation.11 | async-start | bytes 1310720 | tf_op jit(solution)/shard_map/reduce_scatter | solution.py:508
  149.3 15.3 %copy-start.31 = (bf16[2,256,1024]{2,1,0:T(8,128)(2,1)S(1)}, bf16[2,256,1024]{2,1,0:T(8,128)(2,1)}, u32[]{:S(2)}) copy-start(bf16[2,256,1024]{2,1,0:T(8,128)(2,1)} %param.21) | copy-start | bytes 3145732
  167.5 65.3 %reduce-scatter.12.cloned.1.call-start = ((), (), s32[]{:S(2)}) async-start(), calls=%async_computation.12 | async-start | bytes 1310720 | tf_op jit(solution)/shard_map/reduce_scatter | solution.py:518
  194.5 4.2 %copy-start.15 = (bf16[512,4]{1,0:T(8,128)(2,1)S(1)}, bf16[512,4]{1,0:T(8,128)(2,1)}, u32[]{:S(2)}) copy-start(bf16[512,4]{1,0:T(8,128)(2,1)} %get-tuple-element.38) | copy-start | bytes 12292
  200.2 189.4 %reduce-scatter.14.cloned.1.call-start = ((), (), s32[]{:S(2)}) async-start(), calls=%async_computation.13 | async-start | bytes 10027008 | tf_op jit(solution)/shard_map/reduce_scatter | solution.py:536
  233.9 48.9 %copy-start.28 = (f32[128]{0:T(128)S(1)}, f32[128]{0:T(128)}, u32[]{:S(2)}) copy-start(f32[128]{0:T(128)} %copy-done.27) | copy-start | bytes 1540
  233.9 48.9 %copy-start.8 = (bf16[128,1024]{1,0:T(8,128)(2,1)S(1)}, bf16[128,1024]{1,0:T(8,128)(2,1)}, u32[]{:S(2)}) copy-start(bf16[128,1024]{1,0:T(8,128)(2,1)} %param.25) | copy-start | bytes 786436
  233.9 48.9 %copy-start.9 = (bf16[128,1024]{1,0:T(8,128)(2,1)S(1)}, bf16[128,1024]{1,0:T(8,128)(2,1)}, u32[]{:S(2)}) copy-start(bf16[128,1024]{1,0:T(8,128)(2,1)} %reduce-scatter.8.cloned.1.call-done) | copy-start | bytes 786436
  233.9 48.9 %copy-start.16 = (bf16[128,1024]{1,0:T(8,128)(2,1)S(1)}, bf16[128,1024]{1,0:T(8,128)(2,1)}, u32[]{:S(2)}) copy-start(bf16[128,1024]{1,0:T(8,128)(2,1)} %reduce-scatter.10.cloned.1.call-done) | copy-start | bytes 786436
  233.9 48.9 %copy-start.21 = (f32[128]{0:T(128)S(1)}, f32[128]{0:T(128)}, u32[]{:S(2)}) copy-start(f32[128]{0:T(128)} %copy-done.20) | copy-start | bytes 1540
  233.9 48.9 %copy-start.26 = (f32[128]{0:T(128)S(1)}, f32[128]{0:T(128)}, u32[]{:S(2)}) copy-start(f32[128]{0:T(128)} %copy-done.25) | copy-start | bytes 1540
  393.1 6.4 %copy-start.1 = (bf16[1024,2,704]{0,2,1:T(8,128)(2,1)S(1)}, bf16[1024,2,704]{0,2,1:T(8,128)(2,1)}, u32[]{:S(2)}) copy-start(bf16[1024,2,704]{0,2,1:T(8,128)(2,1)} %param.23) | copy-start | bytes 8650756
  (22 other events, 44.4 us)
Sparse Core Ops, SparseCore 0:
  10.4 19.4 all-gather.4
  31.5 16.6 all-gather.6
  66.2 24.8 reduce-scatter.5
  94.1 16.6 all-gather.8
  119.6 24.7 reduce-scatter.7
  147.8 16.6 all-gather.10
  167.6 24.7 reduce-scatter.9
  200.3 24.7 reduce-scatter.11
  234.1 155.4 reduce-scatter.13
